TPU v7x, 32 devices: a whole 2x2x4 slice. The times are simulated.
32 devices in a mesh: batch: 8 (over y, x, core), head: 4 (over z).
Axes of the slice: x: 2, y: 2, z: 4, core: 2. Of those that a mesh axis runs over, the one named last changes fastest.
Arguments:
- layer_input: bfloat16 [16384, 768], P(('batch', 'head')), may hold values from -6 to 6
- memory_flags: int32 [32], P('batch'), may hold values 0 or 1
- document_start: int32 [32], P('batch'), may hold values from 1 to 511
- memory_coefficients: bfloat16 [32, 256, 768], P('batch'), may hold values from -6 to 6
- first_gain: bfloat16 [768], replicated, may hold values from 0.5 to 1.5
- first_shift: bfloat16 [768], replicated, may hold values from -1 to 1
- query_weight: bfloat16 [768, 768], P(None, 'head'), may hold values from -0.3125 to 0.3125
- query_bias: bfloat16 [768], P('head'), may hold values from -1 to 1
- key_matrix: bfloat16 [768, 768], P(None, 'head'), may hold values from -0.21875 to 0.21875
- value_matrix: bfloat16 [768, 768], P(None, 'head'), may hold values from -0.21875 to 0.21875
- value_offset_bias: bfloat16 [768], P('head'), may hold values from -1 to 1
- out_weight: bfloat16 [768, 768], P('head'), may hold values from -0.875 to 0.875
- out_bias: bfloat16 [768], replicated, may hold values from -1 to 1
- second_gain: bfloat16 [768], replicated, may hold values from 0.5 to 1.5
- second_shift: bfloat16 [768], replicated, may hold values from -1 to 1
- up_weight: bfloat16 [768, 3072], P(None, 'head'), may hold values from -0.21875 to 0.21875
- up_bias: bfloat16 [3072], P('head'), may hold values from -1 to 1
- down_weight: bfloat16 [3072, 768], P('head'), may hold values from -0.109375 to 0.109375
- down_bias: bfloat16 [768], replicated, may hold values from -1 to 1
- centre_weight: float32 [12, 256], P('head'), may hold values from -0.375 to 0.375
- width_weight: float32 [12, 256], P('head'), may hold values from -0.375 to 0.375
- grad_output: bfloat16 [16384, 768], P(('batch', 'head')), may hold values from -6 to 6
Outputs:
- layer_output: bfloat16 [16384, 768], P(('batch', 'head'))
- input_grad: bfloat16 [16384, 768], P(('batch', 'head'))
- first_gain_grad: float32 [768], replicated
- first_shift_grad: float32 [768], replicated
- query_weight_grad: float32 [768, 768], P(None, 'head')
- query_bias_grad: float32 [768], P('head')
- key_weight_grad: float32 [768, 768], P(None, 'head')
- value_weight_grad: float32 [768, 768], P(None, 'head')
- value_bias_grad: float32 [768], P('head')
- out_weight_grad: float32 [768, 768], P('head')
- out_bias_grad: float32 [768], replicated
- second_gain_grad: float32 [768], replicated
- second_shift_grad: float32 [768], replicated
- up_weight_grad: float32 [768, 3072], P(None, 'head')
- up_bias_grad: float32 [3072], P('head')
- down_weight_grad: float32 [3072, 768], P('head')
- down_bias_grad: float32 [768], replicated
- centre_weight_grad: float32 [12, 256], P('head')
- width_weight_grad: float32 [12, 256], P('head')
Inputs may be any that keep to these rules, and one draw needn't show every extreme that they name: `memory_flags`: 1 marks a segment with memory.
All inputs are finite; a program needn't handle non-finite values. No bound on the sum of `memory_flags` on one device may be relied on, other than what follows from the above.
Results may differ from a plain program's by a relative error of at most 0.018.
The roundings to bfloat16 on the way count: a program that leaves them out, or rounds other values in their place, can miss the bound.
Values may be sent and summed in bfloat16 or wider, within the bound.
A program may use at most 128 MiB of HBM per device.

v0:
```python
import math

import jax
import jax.numpy as jnp
from jax import lax
from jax.sharding import PartitionSpec as P


def norm_stats(values_in):
    center = values_in - jnp.mean(values_in, axis=-1, keepdims=True)
    factor = lax.rsqrt(jnp.mean(center * center, axis=-1, keepdims=True) + 1e-05)
    return (center * factor, factor)


def norm_back(grad, normed, factor):
    return factor * (
        grad
        - jnp.mean(grad, axis=-1, keepdims=True)
        - normed * jnp.mean(grad * normed, axis=-1, keepdims=True)
    )


def cross_dot(left, right):
    return lax.dot_general(
        left, right, (((0,), (0,)), ((), ())), preferred_element_type=jnp.float32
    )


def back_dot(left, right):
    return lax.dot_general(
        left, right, (((1,), (1,)), ((), ())), preferred_element_type=jnp.float32
    )


def segment_mask(length, bound):
    row_ids = lax.broadcasted_iota(jnp.int32, (length, length), 0)
    col_ids = lax.broadcasted_iota(jnp.int32, (length, length), 1)
    return (col_ids <= row_ids) & ((col_ids >= bound) | (row_ids < bound))


def masked_scores(queries, keys_low, bound):
    factor = queries.shape[-1] ** (-0.5)
    scores = (
        jnp.einsum("qhd,khd->hqk", queries, keys_low, preferred_element_type=jnp.float32) * factor
    )
    return jnp.where(segment_mask(queries.shape[0], bound)[None], scores, -1000000000.0)


def recall_terms(queries, memory_keys, centre_weight, width_weight):
    factor = queries.shape[-1] ** (-0.5)
    mem_scores = (
        jnp.einsum("qhd,nhd->hqn", queries, memory_keys, preferred_element_type=jnp.float32)
        * factor
    )
    centre = jax.nn.sigmoid(
        jnp.einsum("hqn,hn->hq", mem_scores, centre_weight, precision=lax.Precision.HIGHEST)
    )
    width_pre = jnp.einsum("hqn,hn->hq", mem_scores, width_weight, precision=lax.Precision.HIGHEST)
    spread = 0.02 * jax.nn.softplus(width_pre) + 0.01
    basis_count = memory_keys.shape[0]
    centres = (jnp.arange(basis_count, dtype=jnp.float32) + 0.5) / basis_count
    offset = centre[..., None] - centres
    recall = (
        jnp.exp(-offset * offset / (2.0 * spread[..., None]))
        * lax.rsqrt(2.0 * math.pi * spread[..., None])
        / basis_count
    )
    return (mem_scores, centre, width_pre, spread, offset, recall)


def forward_segment(segment_item, centre_weight, width_weight):
    queries, keys_low, values, memory_keys, memory_values, flag, bound = segment_item
    scores = masked_scores(queries, keys_low, bound)
    row_peak = jnp.max(scores, axis=-1, keepdims=True)
    shifted = jnp.exp(scores - row_peak)
    row_total = jnp.sum(shifted, axis=-1, keepdims=True)
    probs_low = (shifted / row_total).astype(jnp.bfloat16)
    local_mix = jnp.einsum("hqk,khd->qhd", probs_low, values, preferred_element_type=jnp.float32)
    recall_low = recall_terms(queries, memory_keys, centre_weight, width_weight)[5].astype(
        jnp.bfloat16
    )
    recalled = jnp.einsum(
        "hqn,nhd->qhd", recall_low, memory_values, preferred_element_type=jnp.float32
    )
    context = (local_mix + flag * recalled).astype(jnp.bfloat16)
    return (context, (row_peak + jnp.log(row_total))[..., 0])


def backward_segment(segment_item, centre_weight, width_weight):
    queries, keys_low, values, memory_keys, memory_values, flag, bound, log_total, grad_context = (
        segment_item
    )
    factor = queries.shape[-1] ** (-0.5)
    scores = masked_scores(queries, keys_low, bound)
    attn_probs = jnp.exp(scores - log_total[..., None])
    probs_low = attn_probs.astype(jnp.bfloat16)
    grad_values = jnp.einsum(
        "hqk,qhd->khd", probs_low, grad_context, preferred_element_type=jnp.float32
    )
    grad_probs = jnp.einsum(
        "qhd,khd->hqk", grad_context, values, preferred_element_type=jnp.float32
    )
    grad_scores = (
        attn_probs * (grad_probs - jnp.sum(attn_probs * grad_probs, axis=-1, keepdims=True))
    ).astype(jnp.bfloat16)
    mem_scores, centre, width_pre, spread, offset, recall = recall_terms(
        queries, memory_keys, centre_weight, width_weight
    )
    recall_low = recall.astype(jnp.bfloat16)
    grad_recall = flag * jnp.einsum(
        "qhd,nhd->hqn", grad_context, memory_values, preferred_element_type=jnp.float32
    )
    memory_value_gradient = flag * jnp.einsum(
        "hqn,qhd->nhd", recall_low, grad_context, preferred_element_type=jnp.float32
    )
    weighted = grad_recall * recall
    spread_b = spread[..., None]
    grad_centre = jnp.sum(weighted * (-offset / spread_b), axis=-1)
    grad_spread = jnp.sum(
        weighted * (offset * offset / (2.0 * spread_b * spread_b) - 0.5 / spread_b), axis=-1
    )
    centre_pre_grad = grad_centre * centre * (1.0 - centre)
    width_pre_grad = grad_spread * 0.02 * jax.nn.sigmoid(width_pre)
    grad_mem_scores = (
        centre_pre_grad[..., None] * centre_weight[:, None, :]
        + width_pre_grad[..., None] * width_weight[:, None, :]
    ).astype(jnp.bfloat16)
    centre_grad = jnp.einsum(
        "hq,hqn->hn", centre_pre_grad, mem_scores, precision=lax.Precision.HIGHEST
    )
    width_grad = jnp.einsum(
        "hq,hqn->hn", width_pre_grad, mem_scores, precision=lax.Precision.HIGHEST
    )
    grad_queries = factor * (
        jnp.einsum("hqk,khd->qhd", grad_scores, keys_low, preferred_element_type=jnp.float32)
        + jnp.einsum(
            "hqn,nhd->qhd", grad_mem_scores, memory_keys, preferred_element_type=jnp.float32
        )
    )
    grad_keys = factor * jnp.einsum(
        "hqk,qhd->khd", grad_scores, queries, preferred_element_type=jnp.float32
    )
    memory_key_gradient = factor * jnp.einsum(
        "hqn,qhd->nhd", grad_mem_scores, queries, preferred_element_type=jnp.float32
    )
    return (
        grad_queries.astype(jnp.bfloat16),
        grad_keys.astype(jnp.bfloat16),
        grad_values.astype(jnp.bfloat16),
        memory_key_gradient.astype(jnp.bfloat16),
        memory_value_gradient.astype(jnp.bfloat16),
        centre_grad,
        width_grad,
    )


def per_device(
    layer_input,
    memory_flags,
    document_start,
    memory_coefficients,
    first_gain,
    first_shift,
    query_weight,
    query_bias,
    key_matrix,
    value_matrix,
    value_offset_bias,
    out_weight,
    out_bias,
    second_gain,
    second_shift,
    up_weight,
    up_bias,
    down_weight,
    down_bias,
    centre_weight,
    width_weight,
    grad_output,
):
    segments = memory_coefficients.shape[0]
    basis_count = memory_coefficients.shape[1]
    group_heads = centre_weight.shape[0]
    group_cols = query_weight.shape[1]
    head_size = group_cols // group_heads
    flag_values = memory_flags.astype(jnp.float32)
    inputs = layer_input.astype(jnp.float32)
    normed_one, factor_one = norm_stats(inputs)
    first_low = (normed_one * first_gain + first_shift).astype(jnp.bfloat16)
    first_rows = lax.all_gather(first_low, "head", axis=0, tiled=True)
    total_rows = first_rows.shape[0]
    length = total_rows // segments
    queries = (
        jnp.dot(first_rows, query_weight, preferred_element_type=jnp.float32) + query_bias
    ).astype(jnp.bfloat16)
    keys_low = jnp.dot(first_rows, key_matrix, preferred_element_type=jnp.float32).astype(
        jnp.bfloat16
    )
    values = (
        jnp.dot(first_rows, value_matrix, preferred_element_type=jnp.float32) + value_offset_bias
    ).astype(jnp.bfloat16)
    memory_keys = jnp.einsum(
        "wmr,rq->wmq", memory_coefficients, key_matrix, preferred_element_type=jnp.float32
    ).astype(jnp.bfloat16)
    memory_values = (
        jnp.einsum(
            "wmr,rq->wmq", memory_coefficients, value_matrix, preferred_element_type=jnp.float32
        )
        + value_offset_bias
    ).astype(jnp.bfloat16)
    tile_shape = (segments, length, group_heads, head_size)
    basis_dimensions = (segments, basis_count, group_heads, head_size)
    seg_items = (
        queries.reshape(tile_shape),
        keys_low.reshape(tile_shape),
        values.reshape(tile_shape),
        memory_keys.reshape(basis_dimensions),
        memory_values.reshape(basis_dimensions),
        flag_values,
        document_start,
    )
    context, log_total = lax.map(
        lambda segment_item: forward_segment(segment_item, centre_weight, width_weight), seg_items
    )
    context = context.reshape(total_rows, group_cols)
    attn_sum = lax.psum_scatter(
        jnp.dot(context, out_weight, preferred_element_type=jnp.float32).astype(jnp.bfloat16),
        "head",
        scatter_dimension=0,
        tiled=True,
    ).astype(jnp.float32)
    hidden = inputs + (attn_sum + out_bias)
    normed_two, factor_two = norm_stats(hidden)
    second_low = (normed_two * second_gain + second_shift).astype(jnp.bfloat16)
    second_rows = lax.all_gather(second_low, "head", axis=0, tiled=True)
    up_pre = jnp.dot(second_rows, up_weight, preferred_element_type=jnp.float32) + up_bias
    up_act = jax.nn.gelu(up_pre, approximate=True).astype(jnp.bfloat16)
    mlp_sum = lax.psum_scatter(
        jnp.dot(up_act, down_weight, preferred_element_type=jnp.float32).astype(jnp.bfloat16),
        "head",
        scatter_dimension=0,
        tiled=True,
    ).astype(jnp.float32)
    layer_output = (hidden + (mlp_sum + down_bias)).astype(jnp.bfloat16)
    down_bias_grad = jnp.sum(grad_output.astype(jnp.float32), axis=0)
    grad_rows = lax.all_gather(grad_output, "head", axis=0, tiled=True)
    down_weight_grad = cross_dot(up_act, grad_rows)
    grad_act = back_dot(grad_rows, down_weight)
    gelu_pull = jax.vjp(lambda values_in: jax.nn.gelu(values_in, approximate=True), up_pre)[1]
    grad_up = gelu_pull(grad_act)[0].astype(jnp.bfloat16)
    up_bias_grad = jnp.sum(grad_up.astype(jnp.float32), axis=0)
    up_weight_grad = cross_dot(second_rows, grad_up)
    grad_second = lax.psum_scatter(
        back_dot(grad_up, up_weight).astype(jnp.bfloat16), "head", scatter_dimension=0, tiled=True
    ).astype(jnp.float32)
    second_gain_grad = jnp.sum(grad_second * normed_two, axis=0)
    second_shift_grad = jnp.sum(grad_second, axis=0)
    grad_hidden = grad_output.astype(jnp.float32) + norm_back(
        grad_second * second_gain, normed_two, factor_two
    )
    branch_low = grad_hidden.astype(jnp.bfloat16)
    out_bias_grad = jnp.sum(branch_low.astype(jnp.float32), axis=0)
    branch_rows = lax.all_gather(branch_low, "head", axis=0, tiled=True)
    out_weight_grad = cross_dot(context, branch_rows)
    grad_context = back_dot(branch_rows, out_weight).astype(jnp.bfloat16)
    back_items = seg_items + (log_total, grad_context.reshape(tile_shape))
    results = lax.map(
        lambda segment_item: backward_segment(segment_item, centre_weight, width_weight), back_items
    )
    grad_queries = results[0].reshape(total_rows, group_cols)
    grad_keys = results[1].reshape(total_rows, group_cols)
    grad_values = results[2].reshape(total_rows, group_cols)
    memory_key_gradient = results[3].reshape(segments, basis_count, group_cols)
    memory_value_gradient = results[4].reshape(segments, basis_count, group_cols)
    centre_weight_grad = jnp.sum(results[5], axis=0)
    width_weight_grad = jnp.sum(results[6], axis=0)
    query_weight_grad = cross_dot(first_rows, grad_queries)
    query_bias_grad = jnp.sum(grad_queries.astype(jnp.float32), axis=0)
    key_weight_grad = cross_dot(first_rows, grad_keys) + jnp.einsum(
        "qwo,qwy->oy", memory_coefficients, memory_key_gradient, preferred_element_type=jnp.float32
    )
    value_weight_grad = cross_dot(first_rows, grad_values) + jnp.einsum(
        "qwo,qwy->oy",
        memory_coefficients,
        memory_value_gradient,
        preferred_element_type=jnp.float32,
    )
    value_bias_grad = jnp.sum(grad_values.astype(jnp.float32), axis=0) + jnp.sum(
        memory_value_gradient.astype(jnp.float32), axis=(0, 1)
    )
    grad_first = lax.psum_scatter(
        (
            back_dot(grad_queries, query_weight)
            + back_dot(grad_keys, key_matrix)
            + back_dot(grad_values, value_matrix)
        ).astype(jnp.bfloat16),
        "head",
        scatter_dimension=0,
        tiled=True,
    ).astype(jnp.float32)
    first_gain_grad = jnp.sum(grad_first * normed_one, axis=0)
    first_shift_grad = jnp.sum(grad_first, axis=0)
    input_grad = (grad_hidden + norm_back(grad_first * first_gain, normed_one, factor_one)).astype(
        jnp.bfloat16
    )
    (
        query_weight_grad,
        query_bias_grad,
        key_weight_grad,
        value_weight_grad,
        value_bias_grad,
        out_weight_grad,
        centre_weight_grad,
        width_weight_grad,
        down_weight_grad,
        up_weight_grad,
        up_bias_grad,
    ) = lax.psum(
        (
            query_weight_grad,
            query_bias_grad,
            key_weight_grad,
            value_weight_grad,
            value_bias_grad,
            out_weight_grad,
            centre_weight_grad,
            width_weight_grad,
            down_weight_grad,
            up_weight_grad,
            up_bias_grad,
        ),
        "batch",
    )
    (
        first_gain_grad,
        first_shift_grad,
        out_bias_grad,
        second_gain_grad,
        second_shift_grad,
        down_bias_grad,
    ) = lax.psum(
        (
            first_gain_grad,
            first_shift_grad,
            out_bias_grad,
            second_gain_grad,
            second_shift_grad,
            down_bias_grad,
        ),
        ("batch", "head"),
    )
    return (
        layer_output,
        input_grad,
        first_gain_grad,
        first_shift_grad,
        query_weight_grad,
        query_bias_grad,
        key_weight_grad,
        value_weight_grad,
        value_bias_grad,
        out_weight_grad,
        out_bias_grad,
        second_gain_grad,
        second_shift_grad,
        up_weight_grad,
        up_bias_grad,
        down_weight_grad,
        down_bias_grad,
        centre_weight_grad,
        width_weight_grad,
    )


def solution(mesh):
    placed = (
        P(("batch", "head"), None),
        P("batch"),
        P("batch"),
        P("batch", None, None),
        P(),
        P(),
        P(None, "head"),
        P("head"),
        P(None, "head"),
        P(None, "head"),
        P("head"),
        P("head", None),
        P(),
        P(),
        P(),
        P(None, "head"),
        P("head"),
        P("head", None),
        P(),
        P("head", None),
        P("head", None),
        P(("batch", "head"), None),
    )
    return jax.shard_map(
        per_device,
        mesh=mesh,
        in_specs=placed,
        out_specs=(
            P(("batch", "head"), None),
            P(("batch", "head"), None),
            P(),
            P(),
            P(None, "head"),
            P("head"),
            P(None, "head"),
            P(None, "head"),
            P("head"),
            P("head", None),
            P(),
            P(),
            P(),
            P(None, "head"),
            P("head"),
            P("head", None),
            P(),
            P("head", None),
            P("head", None),
        ),
        check_vma=False,
    )
```

profile of v0, /device:TPU:1, one launch (start us, length us, event | category | flops | bytes accessed | tf_op | source)
XLA Modules:
  0.0 868.1 jit_solution(15008076573527793442)
XLA Ops:
  14.6 63.3 %all-gather.5.cloned.1.call-done = bf16[2048,768]{1,0:T(8,128)(2,1)} async-done(((bf16[512,768]{1,0:T(8,128)(2,1)}), bf16[2048,768]{1,0:T(8,128)(2,1)}) %all-gather.5.cloned.1.call-update) | async-done | bytes 3145744 | tf_op jit(solution)/shard_map/all_gather | solution.py:190
  78.0 3.1 fusion.166
  83.8 3.9 fusion.165
  87.8 3.4 reshape.257
  91.2 2.2 copy.58
  93.4 4.0 convolution_convert_fusion.4
  97.3 3.0 reshape.259
  100.3 2.2 copy.60
  103.5 54.4 %while.34 = (s32[]{:T(128)}, bf16[4,512,3,64]{1,3,2,0:T(8,128)(2,1)}, f32[4,3,512]{2,1,0:T(4,128)}, bf16[4,512,3,64]{1,3,2,0:T(8,128)(2,1)}, s32[4]{0:T(128)S(1)...) while((s32[]{:T(128)}, ...), condition=%wide.region_5.6_spmd, body=%wide.region_2.5_spmd.sunk | while | flops 325111296 | bytes 17297064 | solution.py:222
  111.3 2.0 fusion.318
  113.9 3.2 fusion.321
  124.9 2.0 fusion.318
  127.5 3.2 fusion.321
  138.5 2.0 fusion.318
  141.1 3.2 fusion.321
  152.1 2.0 fusion.318
  154.7 3.2 fusion.321
  160.8 2.7 convolution_convert_fusion.2
  166.1 56.3 %reduce-scatter.5.cloned.1.call-done = bf16[512,768]{1,0:T(8,128)(2,1)} async-done(((bf16[2048,768]{1,0:T(8,128)(2,1)}), bf16[512,768]{1,0:T(8,128)(2,1)}) %reduce-scatter.5.cloned.1.call-update) | async-done | bytes 786448 | tf_op jit(solution)/shard_map/reduce_scatter | solution.py:226
  228.4 61.9 %all-gather.7.cloned.1.call-done = bf16[2048,768]{1,0:T(8,128)(2,1)} async-done(((bf16[512,768]{1,0:T(8,128)(2,1)}), bf16[2048,768]{1,0:T(8,128)(2,1)}) %all-gather.7.cloned.1.call-update) | async-done | bytes 3145744 | tf_op jit(solution)/shard_map/all_gather | solution.py:235
  290.3 7.5 fusion.196
  297.8 56.1 %all-gather.9.cloned.1.call-done = bf16[2048,768]{1,0:T(8,128)(2,1)} async-done(((bf16[512,768]{1,0:T(8,128)(2,1)}), bf16[2048,768]{1,0:T(8,128)(2,1)}) %all-gather.9.cloned.1.call-update) | async-done | bytes 3145744 | tf_op jit(solution)/shard_map/all_gather | solution.py:246
  353.9 11.0 %convert_reduce_fusion = (f32[768]{0:T(1024)}, bf16[2048,768]{1,0:T(8,128)(2,1)S(1)}, bf16[2048,768]{1,0:T(8,128)(2,1)}) fusion(f32[2048,768]{1,0:T(8,128)} %fusion.196, f32[768]{0:T(1024)} %convert_element_type.193, bf16[2048,768]{1,0:T(8,128)(2,1)} %all-gather.9.cloned.1.call-done, bf16[768,768]{1,0:T(8,128)(2,1)} %param.43), kind=kOutput, calls=%fused_computation.206 | convolution fusion | flops 2455239936 | bytes 16914432 | tf_op jit(solution)/shard_map/dot_general | solution.py:30
  366.5 4.0 convolution_convert_fusion
  370.6 6.5 convolution_convert_fusion.1
  378.5 51.0 %reduce-scatter.9.cloned.1.call-done = bf16[512,768]{1,0:T(8,128)(2,1)} async-done(((bf16[2048,768]{1,0:T(8,128)(2,1)}), bf16[512,768]{1,0:T(8,128)(2,1)}) %reduce-scatter.9.cloned.1.call-update) | async-done | bytes 786448 | tf_op jit(solution)/shard_map/reduce_scatter | solution.py:253
  429.5 2.9 fusion.188
  433.0 59.0 %reduce-scatter.7.cloned.1.call-done = bf16[512,768]{1,0:T(8,128)(2,1)} async-done(((bf16[2048,768]{1,0:T(8,128)(2,1)}), bf16[512,768]{1,0:T(8,128)(2,1)}) %reduce-scatter.7.cloned.1.call-update) | async-done | bytes 786448 | tf_op jit(solution)/shard_map/reduce_scatter | solution.py:238
  492.0 5.3 convert_reduce_fusion.5
  497.4 63.7 %all-gather.11.cloned.1.call-done = bf16[2048,768]{1,0:T(8,128)(2,1)} async-done(((bf16[512,768]{1,0:T(8,128)(2,1)}), bf16[2048,768]{1,0:T(8,128)(2,1)}) %all-gather.11.cloned.1.call-update) | async-done | bytes 3145744 | tf_op jit(solution)/shard_map/all_gather | solution.py:263
  561.1 4.0 convolution_convert_fusion.3
  565.0 3.4 reshape.263
  568.4 2.2 copy.64
  573.5 91.2 %while.35 = (s32[]{:T(128)}, bf16[4,512,3,64]{1,3,2,0:T(8,128)(2,1)}, bf16[4,512,3,64]{1,3,2,0:T(8,128)(2,1)}, bf16[4,512,3,64]{1,3,2,0:T(8,128)(2,1)}, bf16[4,2...) while((s32[]{:T(128)}, ...), condition=%wide.region_17.18_spmd, body=%wide.region_13.17_spmd.sunk | while | flops 795121152 | bytes 42630428 | solution.py:267
  579.6 2.7 fusion.348
  602.4 2.7 fusion.348
  625.1 2.7 fusion.348
  647.9 2.7 fusion.348
  671.3 2.8 add_convert_fusion.3
  674.2 7.1 fusion.201
  681.3 4.2 fusion.200
  701.3 22.2 %all-reduce.1 = (f32[192]{0:T(256)}, f32[192]{0:T(256)}, f32[768]{0:T(1024)}, f32[3,256]{1,0:T(4,128)}, f32[3,256]{1,0:T(4,128)}) all-reduce(f32[192]{0:T(256)} %reduce_sum.229, f32[192]{0:T(256)S(1)} %add.258, f32[768]{0:T(1024)} %get-tuple-element.347, f32[3,256]{1,0:T(4,128)} %reduce_sum.237, ...), channel_id=1, replica_groups=mesh['batch'=8,'head'=4] {'batch'}, use_global_device_ids=true, to_apply=%region_27.28 | all-reduce | flops 2688 | bytes 21504 | tf_op jit(solution)/shard_map/psum | solution.py:318
  723.5 9.6 %reduce-scatter.11.cloned.1.call-done = bf16[512,768]{1,0:T(8,128)(2,1)} async-done(((bf16[2048,768]{1,0:T(8,128)(2,1)}), bf16[512,768]{1,0:T(8,128)(2,1)}) %reduce-scatter.11.cloned.1.call-update) | async-done | bytes 786448 | tf_op jit(solution)/shard_map/reduce_scatter | solution.py:291
  733.1 2.0 fusion.189
  735.1 42.0 %all-reduce = (f32[768]{0:T(1024)}, f32[768]{0:T(1024)}, f32[768]{0:T(1024)}, f32[768]{0:T(1024)}, f32[768]{0:T(1024)}, /*index=5*/f32[768]{0:T(1024)}) all-reduce(f32[768]{0:T(1024)S(1)} %get-tuple-element.260, f32[768]{0:T(1024)S(1)} %get-tuple-element.265, ...), channel_id=1, replica_groups=mesh['batch'=8,'head'=4] {'batch','head'}, use_global_device_ids=true, to_apply=%region_22.23 | all-reduce | flops 4608 | bytes 36864 | tf_op jit(solution)/shard_map/psum | solution.py:341
  777.1 2.9 fusion.182
  780.0 73.0 %all-reduce.5.cloned.1.call-done = (f32[768,192]{0,1:T(8,128)}, f32[768,192]{0,1:T(8,128)}, f32[768,192]{0,1:T(8,128)}, f32[192,768]{1,0:T(8,128)}, f32[768,768]{1,0:T(8,128)}, /*index=5*/f32[768,768]{1,0:T(8,128)}) async-done(((f32[768,192]{0,1:T(8,128)}, f32[768,192]{0,1:T(8,128)}, f32[768,192]{0,1:T(8,128)}, f32[192,768]{1,0:T(8,128)}, f32[768,768]{1,0:T(8,128)}, /*index=5*/f32[768,768]{1,0:T(8,128)}), ...) | async-done | bytes 7077904 | tf_op jit(solution)/shard_map/psum | solution.py:318
  853.0 2.0 copy.222
  (365 shorter events, 170.6 us)
Async XLA Ops:
  7.2 5.2 copy-start
  7.2 3.8 copy-start.1
  7.2 3.1 copy-start.45
  7.2 3.2 copy-start.46
  7.2 70.7 %all-gather.5.cloned.1.call-start = ((), (), s32[]{:S(2)}) async-start(), calls=%async_computation.4 | async-start | bytes 3932160 | tf_op jit(solution)/shard_map/all_gather | solution.py:190
  8.8 3.6 copy-start.50
  8.8 3.6 copy-start.51
  8.8 3.6 copy-start.52
  8.8 3.6 copy-start.26
  12.3 210.1 %reduce-scatter.5.cloned.1.call-start = ((), (), s32[]{:S(2)}) async-start(), calls=%async_computation.5 | async-start | bytes 3932160 | tf_op jit(solution)/shard_map/reduce_scatter | solution.py:226
  100.3 3.2 copy-start.33
  100.3 3.2 copy-start.34
  100.3 3.2 copy-start.53
  157.9 2.9 copy-start.29
  163.5 126.8 %all-gather.7.cloned.1.call-start = ((), (), s32[]{:S(2)}) async-start(), calls=%async_computation.6 | async-start | bytes 3932160 | tf_op jit(solution)/shard_map/all_gather | solution.py:235
  222.4 2.7 copy-start.43
  226.5 127.4 %all-gather.9.cloned.1.call-start = ((), (), s32[]{:S(2)}) async-start(), calls=%async_computation.8 | async-start | bytes 3932160 | tf_op jit(solution)/shard_map/all_gather | solution.py:246
  227.0 202.4 %reduce-scatter.9.cloned.1.call-start = ((), (), s32[]{:S(2)}) async-start(), calls=%async_computation.9 | async-start | bytes 3932160 | tf_op jit(solution)/shard_map/reduce_scatter | solution.py:253
  353.9 12.6 %copy-start.49 = (bf16[768,768]{1,0:T(8,128)(2,1)S(1)}, bf16[768,768]{1,0:T(8,128)(2,1)}, u32[]{:S(2)}) copy-start(bf16[768,768]{1,0:T(8,128)(2,1)} %param.41) | copy-start | bytes 3538948
  370.6 121.4 %reduce-scatter.7.cloned.1.call-start = ((), (), s32[]{:S(2)}) async-start(), calls=%async_computation.7 | async-start | bytes 3932160 | tf_op jit(solution)/shard_map/reduce_scatter | solution.py:238
  377.1 183.9 %all-gather.11.cloned.1.call-start = ((), (), s32[]{:S(2)}) async-start(), calls=%async_computation.10 | async-start | bytes 3932160 | tf_op jit(solution)/shard_map/all_gather | solution.py:263
  497.3 235.8 %reduce-scatter.11.cloned.1.call-start = ((), (), s32[]{:S(2)}) async-start(), calls=%async_computation.11 | async-start | bytes 3932160 | tf_op jit(solution)/shard_map/reduce_scatter | solution.py:291
  570.6 2.9 copy-start.54
  570.6 2.9 copy-start.56
  576.7 3.0 copy-start.11
  599.4 3.0 copy-start.11
  622.2 3.0 copy-start.11
  645.0 3.0 copy-start.11
  666.7 3.5 copy-start.9
  667.6 3.7 copy-start.12
  674.1 178.9 %all-reduce.5.cloned.1.call-start = ((), (), s32[]{:S(2)}) async-start(), calls=%async_computation.12 | async-start | bytes 14155776 | tf_op jit(solution)/shard_map/psum | solution.py:318
  674.2 7.1 copy-start.48
  674.2 7.1 copy-start.58
  681.2 4.2 copy-start.25
  685.4 2.1 copy-start.16
  687.8 2.1 copy-start.2
  687.8 2.3 copy-start.10
  694.9 6.1 copy-start.15
  694.9 38.2 %copy-start.36 = (f32[768]{0:T(1024)S(1)}, f32[768]{0:T(1024)}, u32[]{:S(2)}) copy-start(f32[768]{0:T(1024)} %copy-done.35) | copy-start | bytes 9220
  694.9 38.2 %copy-start.38 = (f32[512]{0:T(512)S(1)}, f32[512]{0:T(512)}, u32[]{:S(2)}) copy-start(f32[512]{0:T(512)} %copy-done.37) | copy-start | bytes 6148
  694.9 38.1 %copy-start.41 = (f32[512]{0:T(512)S(1)}, f32[512]{0:T(512)}, u32[]{:S(2)}) copy-start(f32[512]{0:T(512)} %copy-done.40) | copy-start | bytes 6148
  699.5 35.6 %copy-start.44 = (f32[768]{0:T(1024)S(1)}, f32[768]{0:T(1024)}, u32[]{:S(2)}) copy-start(f32[768]{0:T(1024)} %get-tuple-element.258) | copy-start | bytes 9220
  733.1 44.1 %copy-start.18 = (bf16[512,768]{1,0:T(8,128)(2,1)S(1)}, bf16[512,768]{1,0:T(8,128)(2,1)}, u32[]{:S(2)}) copy-start(bf16[512,768]{1,0:T(8,128)(2,1)} %reduce-scatter.11.cloned.1.call-done) | copy-start | bytes 2359300
  853.0 2.1 copy-start.24
  853.0 2.9 copy-start.23
  853.0 3.7 copy-start.22
  855.0 2.5 copy-start.20
  857.5 2.5 copy-start.19
  (26 other events, 33.4 us)
Sparse Core Ops, SparseCore 0:
  12.4 65.5 all-gather.4
  163.6 58.7 reduce-scatter.4
  226.6 63.6 all-gather.6
  291.7 62.1 all-gather.8
  370.7 58.7 reduce-scatter.8
  431.6 60.2 reduce-scatter.6
  497.4 63.6 all-gather.10
  674.2 58.7 reduce-scatter.10
  738.3 114.6 all-reduce.4
where the time goes:
time: 874 us; the launch traced here: 868 us
  waiting for transfers between devices  495 us (57%)
  matrix products  186 us (21%)
  blocking collectives  64.2 us (7%)
  local copies, waits for them, and re-layouts  60.3 us (7%)
  other arithmetic  46.6 us (5%)
  between operations  14.7 us (2%)
    psum x1, waiting for transfers between devices, per_device(): lax.psum((query_weight_grad, query_bias_grad, key_weight_grad, value_weig...  73 us
    all_gather x1, waiting for transfers between devices, per_device(): branch_rows = lax.all_gather(branch_low, 'head', axis=0, tiled=True)  63.7 us
    all_gather x1, waiting for transfers between devices, per_device(): first_rows = lax.all_gather(first_low, 'head', axis=0, tiled=True)  63.3 us
    all_gather x1, waiting for transfers between devices, per_device(): second_rows = lax.all_gather(second_low, 'head', axis=0, tiled=True)  61.9 us
    reduce_scatter x1, waiting for transfers between devices, per_device(): lax.psum_scatter(jnp.dot(up_act, down_weight, preferred_element_type=jnp....  59 us
    reduce_scatter x1, waiting for transfers between devices, per_device(): lax.psum_scatter(jnp.dot(context, out_weight, preferred_element_type=jnp....  56.3 us
    all_gather x1, waiting for transfers between devices, per_device(): grad_rows = lax.all_gather(grad_output, 'head', axis=0, tiled=True)  56.1 us
    reduce_scatter x1, waiting for transfers between devices, per_device(): lax.psum_scatter(back_dot(grad_up, up_weight).astype(jnp.bfloat16), 'head...  51 us
  transfers between devices with their start and end apart: 9, of which 9 were waited for; matrix products, arithmetic and copies ran while one was open for 6% of the time, Pallas kernels for 0%

commit v1 on v0

v1 whole, which is shorter than its diff:
```python
import math

import jax
import jax.numpy as jnp
from jax import lax
from jax.experimental import pallas as pl
from jax.experimental.pallas import tpu as pltpu
from jax.sharding import PartitionSpec as P

F32 = jnp.float32
BF16 = jnp.bfloat16
EPS = 1e-05
ROOT = math.sqrt(2.0 / math.pi)
CUBE = 0.044715
ROW_TILE = 32


def mm(left, right):
    return lax.dot_general(left, right, (((1,), (0,)), ((), ())), preferred_element_type=F32)


def mm_nt(left, right):
    return lax.dot_general(left, right, (((1,), (1,)), ((), ())), preferred_element_type=F32)


def mm_tn(left, right):
    return lax.dot_general(left, right, (((0,), (0,)), ((), ())), preferred_element_type=F32)


def three_parts(value):
    high = value.astype(BF16)
    rest = value - high.astype(F32)
    middle = rest.astype(BF16)
    low = (rest - middle.astype(F32)).astype(BF16)
    return high, middle, low


def lane_mean(value):
    return jnp.mean(value, axis=-1, keepdims=True)


def norm_rows(value):
    center = value - lane_mean(value)
    factor = lax.rsqrt(lane_mean(center * center) + EPS)
    return center * factor, factor


def fold8(value):
    return jnp.sum(value.reshape(value.shape[0] // 8, 8, value.shape[1]), axis=0)


def row_sum(value):
    return jnp.sum(value, axis=0, keepdims=True)


ATT, OUT, MLP = 0, 1, 2
KINDS = (ATT, OUT, MLP)
MESH = pl.DeviceIdType.MESH
SUB = 8


class Exchange:
    def __init__(self, n_batch, n_head, wa, wm, recv, fin, more, sems):
        self.n_head = n_head
        self.wa, self.wm = wa, wm
        self.recv, self.fin, self.more = recv, fin, more
        (self.ag_s, self.ag_r, self.rs_s, self.rs_r, self.fin_s, self.fin_r, self.ex_s, self.ex_r,
         self.sm_s, self.sm_r, self.ax_s, self.ax_r) = sems
        b, h = lax.axis_index("batch"), lax.axis_index("head")
        self.b, self.h = b, h
        core, x, y = lax.rem(b, 2), lax.rem(lax.div(b, 2), 2), lax.rem(lax.div(b, 4), 2)
        self.core = core
        across_x, across_y = b + 2 - 4 * x, b + 4 - 8 * y
        self.mate = b + 1 - 2 * core
        self.near = across_x + core * (across_y - across_x)
        self.far = across_y + core * (across_x - across_y)
        self.high = y + core * (x - y)
        self.low = x + core * (y - x)
        self.quarter = 2 * self.high + self.low
        self.other_quarter = 2 * self.high + 1 - self.low
        self.extra = []
        step = SUB
        while step < n_batch:
            bit = lax.rem(lax.div(b, step), 2)
            self.extra.append(b + step - 2 * step * bit)
            step *= 2
        self.half_width = wm.shape[-1] // 2
        self.rows = (wa.shape[1] // n_head, wa.shape[1] // n_head, wm.shape[2])
        self.pending = []

    def barrier(self):
        signal = pltpu.get_barrier_semaphore()
        peers = [(p, self.h) for p in [self.mate, self.near, self.far] + self.extra]
        peers += [(self.b, self.group(k)) for k in range(1, self.n_head)]
        for peer in peers:
            pl.semaphore_signal(signal, inc=1, device_id=peer, device_id_type=MESH)
        pl.semaphore_wait(signal, len(peers))

    def group(self, k):
        return lax.rem(self.h + k, self.n_head)

    def cols(self, which):
        return pl.ds(pl.multiple_of(which * self.half_width, 128), self.half_width)

    def view(self, kind, k, start, count, cols):
        g = self.group(k) if k else self.h
        if kind == MLP:
            return self.wm.at[g, :, pl.ds(pl.multiple_of(start, 16), count), cols]
        first, many = (0, 3) if kind == ATT else (3, 1)
        offset = pl.multiple_of(g * self.rows[kind] + start, 16)
        return self.wa.at[pl.ds(first, many), pl.ds(offset, count), cols]

    def part(self, kind, k, pieces, index, cols):
        count = self.rows[kind] // pieces
        return self.view(kind, k, index * count, count, cols)

    def copy(self, src, dst, send, recv, peer):
        return pltpu.make_async_remote_copy(
            src_ref=src, dst_ref=dst, send_sem=send, recv_sem=recv,
            device_id=peer, device_id_type=MESH,
        )

    def gather_start(self, kind):
        own = self.part(kind, 0, 4, self.quarter, self.cols(self.core))
        for j in range(self.n_head - 1, 0, -1):
            self.copy(
                own, own, self.ag_s.at[kind, j, 0], self.ag_r.at[kind, self.n_head - j, 0],
                (self.b, self.group(j)),
            ).start()

    def gather_step(self, kind, k, stage, receive=False):
        mine = self.cols(self.core)
        if stage == 0:
            ref = self.part(kind, k, 4, self.quarter, mine)
            peer = (self.b, self.group(k))
        elif stage == 1:
            which = self.other_quarter if receive else self.quarter
            ref = self.part(kind, k, 4, which, mine)
            peer = (self.near, self.h)
        elif stage == 2:
            ref = self.part(kind, k, 2, 1 - self.high if receive else self.high, mine)
            peer = (self.far, self.h)
        else:
            ref = self.part(kind, k, 1, 0, self.cols(1 - self.core) if receive else mine)
            peer = (self.mate, self.h)
        return self.copy(
            ref, ref, self.ag_s.at[kind, k, stage], self.ag_r.at[kind, k, stage], peer
        )

    def gather_pass(self, kind, k, stage):
        self.gather_step(kind, k, stage - 1, receive=True).wait_recv()
        if stage < 4:
            self.gather_step(kind, k, stage).start()

    def gather_sent(self, kind, k):
        if k == 0:
            own = self.part(kind, 0, 4, self.quarter, self.cols(self.core))
            for j in range(1, self.n_head):
                self.copy(
                    own, own, self.ag_s.at[kind, j, 0], self.ag_r.at[kind, j, 0],
                    (self.b, self.group(j)),
                ).wait_send()
        else:
            for stage in (1, 2, 3):
                self.gather_step(kind, k, stage).wait_send()

    def reduce_step(self, kind, k, stage):
        mine = self.cols(self.core)
        if stage == 0:
            src, peer = self.part(kind, k, 1, 0, self.cols(1 - self.core)), (self.mate, self.h)
        elif stage == 1:
            src, peer = self.part(kind, k, 2, 1 - self.high, mine), (self.far, self.h)
        elif stage == 2:
            src, peer = self.part(kind, k, 4, self.other_quarter, mine), (self.near, self.h)
        else:
            src, peer = self.part(kind, k, 4, self.quarter, mine), (self.b, self.group(k))
        return self.copy(
            src, self.recv[stage][kind].at[k], self.rs_s.at[kind, k, stage],
            self.rs_r.at[kind, k, stage], peer,
        )

    def add_rows(self, kind, k, start, count, received, out=None):
        mine = self.cols(self.core)
        own = self.view(kind, k, start, count, mine)
        target = own if out is None else out
        sources = [buf.at[k, :, pl.ds(pl.multiple_of(start - base, 16), count), :] for buf, base in received]
        kinds = own.shape[0]
        tile = 48

        for t in range(kinds):
            def step(i, state):
                span = pl.ds(pl.multiple_of(i * tile, 16), tile)
                total = own[t, span, :].astype(F32)
                for source in sources:
                    total = total + source[t, span, :].astype(F32)
                target[t, span, :] = total.astype(BF16)
                return state

            lax.fori_loop(0, count // tile, step, 0)

    def reduce_pass(self, kind, k, stage):
        rows = self.rows[kind]
        half, quarter = rows // 2, rows // 4
        first, second, third = (self.recv[s][kind] for s in range(3))
        if stage > 0:
            self.reduce_step(kind, k, stage - 1).wait_recv()
        kept = self.high * half
        if stage == 1:
            self.add_rows(kind, k, (1 - self.high) * half, half, [(first, 0)])
        elif stage == 2:
            self.add_rows(
                kind, k, self.other_quarter * quarter, quarter, [(first, 0), (second, kept)]
            )
        elif stage == 3:
            own = self.quarter * quarter
            self.add_rows(
                kind, k, own, quarter, [(first, 0), (second, kept), (third, own)]
            )
        if stage < 3 or k > 0:
            self.reduce_step(kind, k, stage).start()

    def fin_part(self, kind, pieces, index, cols):
        count = self.rows[kind] // pieces
        return self.fin[kind].at[:, pl.ds(pl.multiple_of(index * count, 16), count), cols]

    def final_step(self, kind, stage, receive=False):
        mine = self.cols(self.core)
        if stage == 0:
            which = self.other_quarter if receive else self.quarter
            ref, peer = self.fin_part(kind, 4, which, mine), (self.near, self.h)
        elif stage == 1:
            which = 1 - self.high if receive else self.high
            ref, peer = self.fin_part(kind, 2, which, mine), (self.far, self.h)
        else:
            ref = self.fin_part(kind, 1, 0, self.cols(1 - self.core) if receive else mine)
            peer = (self.mate, self.h)
        return self.copy(ref, ref, self.fin_s.at[kind, stage], self.fin_r.at[kind, stage], peer)

    def final_pass(self, kind, stage):
        if stage == 0:
            for k in range(1, self.n_head):
                self.reduce_step(kind, k, 3).wait_recv()
            quarter = self.rows[kind] // 4
            last = self.recv[3][kind]
            mine = self.cols(self.core)
            own = self.view(kind, 0, self.quarter * quarter, quarter, mine)
            target = self.fin_part(kind, 4, self.quarter, mine)
            tile = 48
            for t in range(own.shape[0]):
                def step(i, state):
                    span = pl.ds(pl.multiple_of(i * tile, 16), tile)
                    total = own[t, span, :].astype(F32)
                    for k in range(1, self.n_head):
                        total = total + last[k, t, span, :].astype(F32)
                    target[t, span, :] = total.astype(BF16)
                    return state

                lax.fori_loop(0, quarter // tile, step, 0)
            for e, peer in enumerate(self.extra):
                copy = self.copy(
                    target, self.more[kind].at[e], self.ex_s.at[kind, e], self.ex_r.at[kind, e],
                    (peer, self.h),
                )
                copy.start()
                copy.wait()
                for t in range(own.shape[0]):
                    total = target[t].astype(F32) + self.more[kind][e, t].astype(F32)
                    target[t] = total.astype(BF16)
        else:
            self.final_step(kind, stage - 1, receive=True).wait_recv()
        if stage < 3:
            self.final_step(kind, stage).start()

    def all_sent(self):
        for kind in KINDS:
            for k in range(self.n_head):
                for stage in range(4):
                    if stage < 3 or k > 0:
                        self.reduce_step(kind, k, stage).wait_send()
            for stage in range(3):
                self.final_step(kind, stage).wait_send()

    def aux_copy(self, aux, j):
        own = aux.at[self.h]
        return self.copy(
            own, own, self.ax_s.at[j], self.ax_r.at[self.n_head - j], (self.b, self.group(j))
        )

    def aux_wait(self, aux, k):
        own = aux.at[self.group(k)]
        self.copy(own, own, self.ax_s.at[k], self.ax_r.at[k], (self.b, self.group(k))).wait_recv()

    def small_sum(self, small, got, all_heads):
        for e, peer in enumerate([self.mate, self.near, self.far] + self.extra):
            copy = self.copy(small, got.at[e], self.sm_s.at[e], self.sm_r.at[e], (peer, self.h))
            copy.start()
            copy.wait()
            small[...] = small[...] + got[e]
        first = 3 + len(self.extra)
        copies = []
        for j in range(1, self.n_head):
            copy = self.copy(
                small, all_heads.at[self.h], self.sm_s.at[first + j],
                self.sm_r.at[first + j], (self.b, self.group(j)),
            )
            copy.start()
            copies.append(copy)
        all_heads[self.h] = small[...]
        for copy in copies:
            copy.wait()
        total = all_heads[0]
        for g in range(1, self.n_head):
            total = total + all_heads[g]
        small[...] = total


def schedule(n_head, gp, rp, fp):
    others = range(1, n_head)
    forward = {
        0: [(gp, OUT, k, 1) for k in others] + [(gp, MLP, 1, 1)],
        1: [(gp, OUT, k, 2) for k in others] + [(gp, MLP, 1, 2)],
        2: [(gp, OUT, k, 3) for k in others] + [(gp, MLP, 2, 1)],
        3: [(gp, MLP, 1, 3), (gp, MLP, 2, 2), (gp, MLP, 3, 1)],
        4: [(gp, MLP, 2, 3), (gp, MLP, 3, 2)],
        5: [(gp, MLP, 3, 3)],
    }
    units = {
        1: [(rp, MLP, 0, 1)],
        2: [(rp, MLP, 0, 2), (rp, MLP, 1, 1)],
        3: [(rp, MLP, 0, 3), (rp, MLP, 1, 2)],
    }
    backward = {
        0: [(rp, MLP, 2, 1), (rp, MLP, 1, 3)],
        1: [(rp, MLP, 2, 2), (rp, MLP, 3, 1)],
        2: [(rp, MLP, 2, 3)] + [(rp, OUT, k, 1) for k in range(n_head)],
        3: [(rp, MLP, 3, 2)] + [(rp, OUT, k, 2) for k in range(n_head)],
        4: [(rp, MLP, 3, 3)] + [(rp, OUT, k, 3) for k in range(n_head)],
        5: [(fp, MLP, 0), (fp, OUT, 0), (fp, MLP, 1), (fp, OUT, 1), (fp, MLP, 2), (fp, OUT, 2)],
    }
    return forward, units, backward


def layer_kernel(
    n_batch, n_head,
    flags, bounds, x_in, go_in, mc_in, att_in, up_in, down_in, aux_in, norm_in,
    y_out, dx_out, dqkv_out, dout_out, dmlp_out, small_out,
    xs, gos, mcs, wa, wm, aux, nrm,
    xl, qs, ks, vs, mks, mvs, ctx, prob_top, prob_low, hid, x2, acc, dx2,
    u_s, g_s, act_s, du_s, rt_s,
    cwm, um, cen, spr, wsg, isp, nrs, pg, small,
    got, all_heads, recv, fin, more, links, sems,
):
    gcs, dqs, dks, dvs, gmk, gmv = x2, acc, ks, vs, mks, mvs
    me = lax.axis_index("head")
    rows, width = xs.shape
    heads = prob_low.shape[0]
    blocks = 2
    blk = rows // blocks
    probs = (prob_top, prob_low)
    mask = dx2.at[:, 0:rows]
    s_s = g_s.at[blk:rows, 0:rows]
    ds_s = act_s.at[:, 0:rows]
    pairs = heads // 2
    basis = mcs.shape[0]
    gcols = width // n_head
    tiles = rows // ROW_TILE

    def load(src, dst, index):
        copy = pltpu.make_async_copy(src, dst, sems.at[index])
        copy.start()
        return copy

    net = Exchange(n_batch, n_head, wa, wm, recv, fin, more, links)
    att_copies = [load(att_in, wa.at[:, pl.ds(pl.multiple_of(me * gcols, 16), gcols), :], 5)]
    aux_own = load(aux_in, aux.at[me], 3)
    copies = [
        load(x_in, xs, 0),
        load(norm_in, nrm, 1),
        load(mc_in.at[me], mcs, 2),
        load(go_in, gos, 4),
    ]
    mlp_copies = [load(up_in, wm.at[me, 0], 6), load(down_in, wm.at[me, 1], 7)]
    net.barrier()
    for copy in att_copies:
        copy.wait()
    net.gather_start(ATT)
    aux_own.wait()
    for j in range(1, n_head):
        net.aux_copy(aux, j).start()
    net.gather_start(OUT)
    for copy in mlp_copies:
        copy.wait()
    net.gather_start(MLP)

    flag = flags[me].astype(F32)
    bound = bounds[me]

    def each_tile(body, carry=0):
        def step(i, state):
            return body(pl.ds(pl.multiple_of(i * ROW_TILE, ROW_TILE), ROW_TILE), state)

        return lax.fori_loop(0, tiles, step, carry)

    small[...] = jnp.zeros_like(small)
    zero_sum = jnp.zeros((8, width), F32)

    def mask_rows(span, state):
        row_ids = lax.broadcasted_iota(jnp.int32, (ROW_TILE, rows), 0) + span.start
        col_ids = lax.broadcasted_iota(jnp.int32, (ROW_TILE, rows), 1)
        least = jnp.where(row_ids < bound, 0, bound)
        allowed = (col_ids <= row_ids) & (col_ids >= least)
        mask[span, :] = jnp.where(allowed, 0.0, -jnp.inf).astype(F32)
        return state

    each_tile(mask_rows)
    for copy in copies:
        copy.wait()

    def first_norm(span, state):
        normed, _ = norm_rows(xs[span, :].astype(F32))
        xl[span, :] = (normed * nrm[0:1, :] + nrm[1:2, :]).astype(BF16)
        return state

    each_tile(first_norm)
    for stage in (1, 2, 3, 4):
        for k in range(1, n_head):
            net.gather_pass(ATT, k, stage)
    for k in range(1, n_head):
        net.aux_wait(aux, k)

    tile_n = 256
    for kind, out, mem_out, bias_row in ((0, qs, None, 0), (1, ks, mks, None), (2, vs, mvs, 1)):
        for n in range(0, width, tile_n):
            cols = slice(n, n + tile_n)
            weight = wa[kind, cols, :]
            value = mm_nt(xl[...], weight)
            if bias_row is not None:
                bias = aux[0, bias_row : bias_row + 1, cols]
                for g in range(1, n_head):
                    bias = bias + aux[g, bias_row : bias_row + 1, cols]
                value = value + bias
            out[:, cols] = value.astype(BF16)
            if mem_out is not None:
                value = mm_nt(mcs[...], weight)
                if bias_row is not None:
                    value = value + bias
                mem_out[:, cols] = value.astype(BF16)

    cwm[...] = jnp.zeros_like(cwm)
    per_group = heads // n_head
    for h in range(heads):
        g, k = divmod(h, per_group)
        cwm[h : h + 1, :] = aux[g, 3:4, k * basis : (k + 1) * basis]
        cwm[16 + h : 17 + h, :] = aux[g, 4:5, k * basis : (k + 1) * basis]
    head_width = width // heads
    own_lanes = (
        lax.broadcasted_iota(jnp.int32, (32, width), 0) % 16
        == lax.broadcasted_iota(jnp.int32, (32, width), 1) // head_width
    )
    scale = head_width ** (-0.5)
    parts = three_parts(cwm[...])
    maps = sum(mm(part, mks[...]) for part in reversed(parts))
    maps = jnp.where(own_lanes, maps * scale, 0.0)
    for index, part in enumerate(three_parts(maps)):
        um[32 * index : 32 * index + 32, :] = part
    pre = mm_nt(um[...], qs[...])
    pre = (pre[64:96] + pre[32:64]) + pre[0:32]
    centre = jax.nn.sigmoid(pre[0:16])
    width_pre = pre[16:32]
    spread = 0.02 * (jnp.maximum(width_pre, 0.0) + jnp.log1p(jnp.exp(-jnp.abs(width_pre)))) + 0.01
    cen[...] = centre
    spr[...] = spread
    wsg[...] = jax.nn.sigmoid(width_pre)
    isp[...] = -0.5 / spread
    nrs[...] = lax.rsqrt((2.0 * math.pi) * spread) / basis
    pg[...] = jnp.zeros_like(pg)

    lane = lax.broadcasted_iota(jnp.int32, (1, 2 * head_width), 1)
    half = [
        jnp.where((lane >= head_width) == bool(e), 1.0, 0.0).astype(BF16) for e in range(2)
    ]
    n_tile = 64
    sub = 64

    def recall_tile(head, start):
        ids = lax.broadcasted_iota(jnp.int32, (n_tile, rows), 0).astype(F32)
        offset = cen[pl.ds(head, 1), :] - (ids + (start + 0.5)) / basis
        value = jnp.exp(offset * offset * isp[pl.ds(head, 1), :]) * nrs[pl.ds(head, 1), :]
        return offset, value

    def at(index, slots):
        for value, events in slots.items():
            @pl.when(index == value)
            def _():
                for event, *rest in events:
                    event(*rest)

    gp, rp, fp = net.gather_pass, net.reduce_pass, net.final_pass
    forward_slots, unit_slots, backward_slots = schedule(n_head, gp, rp, fp)

    def forward_pair(p, state):
        at(p, forward_slots)
        lanes = pl.ds(pl.multiple_of(p * 2 * head_width, 2 * head_width), 2 * head_width)
        keys = ks[:, lanes]
        vals = vs[:, lanes]
        queries = qs[:, lanes] * jnp.asarray(scale, BF16)
        mem_vals = mvs[:, lanes] * flag.astype(BF16)
        for e in range(2):
            head = 2 * p + e
            masked_q = queries * half[e]
            masked_v = vals * half[e]
            for r in range(blocks):
                cols = (r + 1) * blk
                s_s[:, :cols] = mm_nt(masked_q[r * blk : (r + 1) * blk], keys[:cols])
                for t in range(0, blk, sub):
                    scores = s_s[t : t + sub, :cols] + mask[r * blk + t : r * blk + t + sub, :cols]
                    shifted = jnp.exp(scores - jnp.max(scores, axis=-1, keepdims=True))
                    inverse = 1.0 / jnp.sum(shifted, axis=-1, keepdims=True)
                    probs[r][head, t : t + sub, :] = (shifted * inverse).astype(BF16)
            for t in range(0, basis, n_tile):
                _, value = recall_tile(head, t)
                rt_s[t : t + n_tile, :] = value.astype(BF16)
            part = mm_tn(rt_s[...], mem_vals * half[e])
            for r in range(blocks):
                cols = (r + 1) * blk
                span = slice(r * blk, (r + 1) * blk)
                value = mm(probs[r][head], masked_v[:cols]) + part[span]
                if e == 0:
                    u_s[span, 0 : 2 * head_width] = value
                else:
                    ctx[span, lanes] = (value + u_s[span, 0 : 2 * head_width]).astype(BF16)
        return state

    lax.fori_loop(0, pairs, forward_pair, 0)

    for k in range(1, n_head):
        gp(OUT, k, 4)

    for n in range(0, width, tile_n):
        hid[:, n : n + tile_n] = mm(ctx[...], wa[3, :, n : n + tile_n])

    def second_norm(span, state):
        hidden = xs[span, :].astype(F32) + (hid[span, :] + nrm[2:3, :])
        hid[span, :] = hidden
        normed, _ = norm_rows(hidden)
        x2[span, :] = (normed * nrm[3:4, :] + nrm[4:5, :]).astype(BF16)
        acc[span, :] = jnp.zeros((ROW_TILE, width), F32)
        dx2[span, :] = jnp.zeros((ROW_TILE, width), F32)
        return state

    each_tile(second_norm)

    def units(k, state):
        g = lax.rem(me + k, n_head)
        at(k, {i: [(gp, MLP, i, 4)] for i in range(1, n_head)})
        for n in range(0, width, tile_n):
            cols = slice(n, n + tile_n)
            u_s[:, cols] = mm(x2[...], wm[g, 0, :, cols])
            g_s[:, cols] = mm_nt(gos[...], wm[g, 1, cols, :])
        bias = aux[g, 2:3, :]

        def activate(span, total):
            pre = u_s[span, :] + bias
            square = pre * pre
            tanh = jnp.tanh(ROOT * pre * (1.0 + CUBE * square))
            outer = 0.5 + 0.5 * tanh
            act_s[span, :] = (pre * outer).astype(BF16)
            slope = outer + (0.5 * ROOT) * pre * (1.0 - tanh * tanh) * (1.0 + (3 * CUBE) * square)
            low = (g_s[span, :] * slope).astype(BF16)
            du_s[span, :] = low
            return total + fold8(low.astype(F32))

        total = each_tile(activate, zero_sum)
        at(k, unit_slots)
        small[pl.ds(8 + g, 1), :] = row_sum(total)
        for n in range(0, width, tile_n):
            cols = slice(n, n + tile_n)
            acc[:, cols] += mm(act_s[...], wm[g, 1, :, cols])
            dx2[:, cols] += mm_nt(du_s[...], wm[g, 0, cols, :])
        at(k, {i: [(net.gather_sent, MLP, i)] for i in range(n_head)})
        for n in range(0, width, tile_n):
            cols = slice(n, n + tile_n)
            wm[g, 1, :, cols] = mm_tn(act_s[...], gos[:, cols]).astype(BF16)
            wm[g, 0, :, cols] = mm_tn(x2[...], du_s[:, cols]).astype(BF16)
        at(k, {i: [(rp, MLP, i, 0)] for i in range(n_head)})
        return state

    lax.fori_loop(0, n_head, units, 0)

    def second_back(span, sums):
        hidden = hid[span, :]
        normed, factor = norm_rows(hidden)
        grad = dx2[span, :]
        grad_out = gos[span, :].astype(F32)
        xl2 = hidden + (acc[span, :] + nrm[5:6, :])
        du_s[span, :] = xl2.astype(BF16)
        scaled = grad * nrm[3:4, :]
        total = grad_out + factor * (
            scaled - lane_mean(scaled) - normed * lane_mean(scaled * normed)
        )
        hid[span, :] = total
        low = total.astype(BF16)
        act_s[span, :] = low
        return (
            sums[0] + fold8(grad * normed),
            sums[1] + fold8(grad),
            sums[2] + fold8(low.astype(F32)),
            sums[3] + fold8(grad_out),
        )

    sums = each_tile(second_back, (zero_sum,) * 4)
    y_copy = load(du_s, y_out, 0)
    small[3:4, :] = row_sum(sums[0])
    small[4:5, :] = row_sum(sums[1])
    small[2:3, :] = row_sum(sums[2])
    small[5:6, :] = row_sum(sums[3])
    for n in range(0, width, tile_n):
        cols = slice(n, n + tile_n)
        gcs[:, cols] = mm_nt(act_s[...], wa[3, cols, :]).astype(BF16)
    for k in range(n_head):
        net.gather_sent(OUT, k)
    for n in range(0, width, tile_n):
        cols = slice(n, n + tile_n)
        wa[3, :, cols] = mm_tn(ctx[...], act_s[:, cols]).astype(BF16)
    for k in range(n_head):
        rp(OUT, k, 0)

    def backward_pair(p, state):
        at(p, backward_slots)
        lanes = pl.ds(pl.multiple_of(p * 2 * head_width, 2 * head_width), 2 * head_width)
        keys = ks[:, lanes]
        vals = vs[:, lanes]
        queries = qs[:, lanes] * jnp.asarray(scale, BF16)
        grads = gcs[:, lanes]
        mem_vals = mvs[:, lanes] * flag.astype(BF16)
        for e in range(2):
            head = 2 * p + e
            masked_g = grads * half[e]
            masked_q = queries * half[e]
            masked_k = keys * half[e]
            for r in range(blocks):
                cols = (r + 1) * blk
                span = slice(r * blk, (r + 1) * blk)
                s_s[:, :cols] = mm_nt(masked_g[span], vals[:cols])
                for t in range(0, blk, sub):
                    inner = slice(r * blk + t, r * blk + t + sub)
                    grad = s_s[t : t + sub, :cols]
                    prob = probs[r][head, t : t + sub, :].astype(F32)
                    total = jnp.sum(prob * grad, axis=-1, keepdims=True)
                    ds_s[inner, :cols] = (prob * (grad - total)).astype(BF16)
                value = mm(ds_s[span, :cols], masked_k[:cols])
                if e == 0:
                    dqs[span, lanes] = value
                else:
                    dqs[span, lanes] += value
            for c in range(blocks):
                span = slice(c * blk, (c + 1) * blk)
                key_part = mm_tn(ds_s[c * blk :, span], masked_q[c * blk :])
                val_part = mm_tn(prob_low[head, :, span], masked_g[blk:])
                if c == 0:
                    val_part = val_part + mm_tn(prob_top[head], masked_g[:blk])
                if e == 0:
                    u_s[span, 0:128] = key_part
                    u_s[span, 128:256] = val_part
                else:
                    dks[span, lanes] = (key_part + u_s[span, 0:128]).astype(BF16)
                    dvs[span, lanes] = (val_part + u_s[span, 128:256]).astype(BF16)
            g_s[0:basis, 0:rows] = mm_nt(mem_vals * half[e], grads)
            sum0 = jnp.zeros((8, rows), F32)
            sum1 = sum0
            sum2 = sum0
            for t in range(0, basis, n_tile):
                offset, value = recall_tile(head, t)
                rt_s[t : t + n_tile, :] = value.astype(BF16)
                weighted = g_s[t : t + n_tile, 0:rows] * value
                moment = weighted * offset
                sum0 = sum0 + fold8(weighted)
                sum1 = sum1 + fold8(moment)
                sum2 = sum2 + fold8(moment * offset)
            part = mm(rt_s[...], masked_g * flag.astype(BF16))
            if e == 0:
                u_s[0:basis, 256:384] = part
            else:
                gmv[:, lanes] = (part + u_s[0:basis, 256:384]).astype(BF16)
            one = pl.ds(head, 1)
            centre = cen[one, :]
            inverse = 1.0 / spr[one, :]
            grad_centre = -row_sum(sum1) * inverse
            grad_spread = (row_sum(sum2) * inverse - row_sum(sum0)) * (0.5 * inverse)
            pg[one, :] = grad_centre * centre * (1.0 - centre)
            pg[pl.ds(16 + head, 1), :] = 0.02 * grad_spread * wsg[one, :]
        return state

    lax.fori_loop(0, pairs, backward_pair, 0)
    y_copy.wait()

    slopes = three_parts(pg[...])
    moments = sum(mm(part, qs[...]) for part in reversed(slopes))
    moments = jnp.where(own_lanes, moments * scale, 0.0)
    pieces = three_parts(moments)
    weight_grads = sum(mm_nt(piece, mks[...]) for piece in reversed(pieces))
    for h in range(heads):
        g, k = divmod(h, per_group)
        small[12 + g : 13 + g, k * basis : (k + 1) * basis] = weight_grads[h : h + 1, :]
        small[16 + g : 17 + g, k * basis : (k + 1) * basis] = weight_grads[16 + h : 17 + h, :]
    gmk[...] = (
        (mm_tn(parts[1], pieces[0]) + mm_tn(parts[0], pieces[1])) + mm_tn(parts[0], pieces[0])
    ).astype(BF16)
    for n in range(0, width, tile_n):
        cols = slice(n, n + tile_n)
        high = um[0:32, cols]
        value = (mm_tn(slopes[1], high) + mm_tn(slopes[0], um[32:64, cols])) + mm_tn(
            slopes[0], high
        )
        act_s[:, cols] = (dqs[:, cols] * scale + value).astype(BF16)
    def bias_sums(span, sums):
        return (
            sums[0] + fold8(act_s[span, :].astype(F32)),
            sums[1] + fold8(dvs[span, :].astype(F32)),
        )

    sums = each_tile(bias_sums, (zero_sum,) * 2)
    small[6:7, :] = row_sum(sums[0])
    small[7:8, :] = row_sum(sums[1]) + row_sum(gmv[...].astype(F32))

    for n in range(0, width, tile_n):
        cols = slice(n, n + tile_n)
        dx2[:, cols] = (
            mm(act_s[...], wa[0, :, cols])
            + mm(dks[...], wa[1, :, cols])
            + mm(dvs[...], wa[2, :, cols])
        )
    for k in range(n_head):
        net.gather_sent(ATT, k)
    for n in range(0, width, tile_n):
        cols = slice(n, n + tile_n)
        wa[0, :, cols] = mm_tn(act_s[...], xl[:, cols]).astype(BF16)
        wa[1, :, cols] = (
            mm_tn(dks[...], xl[:, cols]) + mm_tn(gmk[...], mcs[:, cols])
        ).astype(BF16)
        wa[2, :, cols] = (
            mm_tn(dvs[...], xl[:, cols]) + mm_tn(gmv[...], mcs[:, cols])
        ).astype(BF16)

    for k in range(n_head):
        rp(ATT, k, 0)
    for k in range(n_head):
        rp(ATT, k, 1)

    def first_back(span, sums):
        normed, factor = norm_rows(xs[span, :].astype(F32))
        grad = dx2[span, :]
        scaled = grad * nrm[0:1, :]
        total = hid[span, :] + factor * (
            scaled - lane_mean(scaled) - normed * lane_mean(scaled * normed)
        )
        du_s[span, :] = total.astype(BF16)
        return (sums[0] + fold8(grad * normed), sums[1] + fold8(grad))

    sums = each_tile(first_back, (zero_sum,) * 2)
    small[0:1, :] = row_sum(sums[0])
    small[1:2, :] = row_sum(sums[1])
    outs = [load(du_s, dx_out, 0)]
    for k in range(n_head):
        rp(ATT, k, 2)
    net.small_sum(small, got, all_heads)
    outs += [load(small, small_out, 1)]
    for k in range(n_head):
        rp(ATT, k, 3)
    fp(MLP, 3)
    outs += [load(fin[MLP], dmlp_out, 2)]
    fp(OUT, 3)
    outs += [load(fin[OUT], dout_out, 3)]
    for stage in range(4):
        fp(ATT, stage)
    outs += [load(fin[ATT], dqkv_out, 4)]
    net.all_sent()
    for j in range(1, n_head):
        net.aux_copy(aux, j).wait_send()
    for copy in outs:
        copy.wait()


def per_device(
    n_batch, n_head,
    layer_input, memory_flags, document_start, memory_coefficients,
    first_gain, first_shift, query_weight, query_bias, key_matrix, value_matrix,
    value_offset_bias, out_weight, out_bias, second_gain, second_shift,
    up_weight, up_bias, down_weight, down_bias, centre_weight, width_weight, grad_output,
):
    rows, width = layer_input.shape
    basis = memory_coefficients.shape[1]
    gcols = query_weight.shape[1]
    heads = centre_weight.shape[0] * n_head
    me = lax.axis_index("head")
    att = jnp.stack([query_weight.T, key_matrix.T, value_matrix.T, out_weight])

    def spread(vector):
        return lax.dynamic_update_slice(jnp.zeros((width,), F32), vector.astype(F32), (me * gcols,))

    aux = jnp.stack(
        [spread(query_bias), spread(value_offset_bias), up_bias.astype(F32),
         centre_weight.reshape(width), width_weight.reshape(width)]
    )
    aux = jnp.pad(aux, ((0, 3), (0, 0)))
    norm = jnp.stack(
        [first_gain, first_shift, out_bias, second_gain, second_shift, down_bias]
    ).astype(F32)
    norm = jnp.pad(norm, ((0, 2), (0, 0)))
    extra = 0
    while SUB << extra < n_batch:
        extra += 1

    def vm(*shape, dtype=BF16):
        return pltpu.VMEM(shape, dtype)

    any_spec = pl.BlockSpec(memory_space=pl.ANY)
    smem = pl.BlockSpec(memory_space=pltpu.SMEM)
    dma = pltpu.SemaphoreType.DMA
    halves = ((3, gcols), (1, gcols), (2, width))
    recv = tuple(
        tuple(vm(n_head, t, r // pieces, width // 2) for t, r in halves) for pieces in (1, 2, 4, 4)
    )
    y, dx, dqkv, dout, dmlp, small = pl.pallas_call(
        lambda *refs: layer_kernel(n_batch, n_head, *refs),
        out_shape=(
            jax.ShapeDtypeStruct((rows, width), BF16),
            jax.ShapeDtypeStruct((rows, width), BF16),
            jax.ShapeDtypeStruct((3, gcols, width), BF16),
            jax.ShapeDtypeStruct((1, gcols, width), BF16),
            jax.ShapeDtypeStruct((2, width, width), BF16),
            jax.ShapeDtypeStruct((24, width), F32),
        ),
        in_specs=[smem, smem] + [any_spec] * 8,
        out_specs=[any_spec] * 6,
        scratch_shapes=[
            vm(rows, width), vm(rows, width), vm(basis, width),
            vm(4, width, width), vm(n_head, 2, width, width),
            vm(n_head, 8, width, dtype=F32), vm(8, width, dtype=F32),
            vm(rows, width), vm(rows, width), vm(rows, width), vm(rows, width),
            vm(basis, width), vm(basis, width), vm(rows, width),
            vm(heads, rows // 2, rows // 2), vm(heads, rows // 2, rows),
            vm(rows, width, dtype=F32), vm(rows, width),
            vm(rows, width, dtype=F32), vm(rows, width, dtype=F32),
            vm(rows, width, dtype=F32), vm(rows, width, dtype=F32),
            vm(rows, width), vm(rows, width), vm(basis, rows),
            vm(32, basis, dtype=F32), vm(96, width),
            vm(16, rows, dtype=F32), vm(16, rows, dtype=F32), vm(16, rows, dtype=F32),
            vm(16, rows, dtype=F32), vm(16, rows, dtype=F32), vm(32, rows, dtype=F32),
            vm(24, width, dtype=F32),
            vm(3 + extra, 24, width, dtype=F32), vm(n_head, 24, width, dtype=F32),
            recv,
            tuple(vm(t, r, width) for t, r in halves),
            tuple(vm(extra, t, r // 4, width // 2) for t, r in halves) if extra else (),
            (dma((3, n_head, 4)), dma((3, n_head, 4)), dma((3, n_head, 4)), dma((3, n_head, 4)),
             dma((3, 3)), dma((3, 3)), dma((3, max(extra, 1))), dma((3, max(extra, 1))),
             dma((3 + extra + n_head,)),
             dma((3 + extra + n_head,)), dma((n_head,)), dma((n_head,))),
            dma((8,)),
        ],
        compiler_params=pltpu.CompilerParams(
            collective_id=0, has_side_effects=True, vmem_limit_bytes=67043328
        ),
    )(memory_flags, document_start, layer_input, grad_output, memory_coefficients,
      att, up_weight, down_weight, aux, norm)
    per_group = heads // n_head
    mine = lambda row: lax.dynamic_slice(small[row], (me * gcols,), (gcols,))
    unit = lambda first: lax.dynamic_slice(small, (first + me, 0), (1, width))
    return (
        y, dx, small[0], small[1],
        dqkv[0].T.astype(F32), mine(6), dqkv[1].T.astype(F32), dqkv[2].T.astype(F32), mine(7),
        dout[0].astype(F32),
        small[2], small[3], small[4],
        dmlp[0].astype(F32), unit(8).reshape(width), dmlp[1].astype(F32), small[5],
        unit(12).reshape(per_group, basis), unit(16).reshape(per_group, basis),
    )


def solution(mesh):
    n_batch, n_head = mesh.shape["batch"], mesh.shape["head"]
    tokens = P(("batch", "head"), None)
    cols, rows, split, whole = P(None, "head"), P("head", None), P("head"), P()
    placed = (
        tokens, P("batch"), P("batch"), P("batch", None, None), whole, whole, cols, split, cols,
        cols, split, rows, whole, whole, whole, cols, split, rows, whole, rows, rows, tokens,
    )
    outs = (
        tokens, tokens, whole, whole, cols, split, cols, cols, split, rows, whole, whole, whole,
        cols, split, rows, whole, rows, rows,
    )
    return jax.shard_map(
        lambda *args: per_device(n_batch, n_head, *args),
        mesh=mesh, in_specs=placed, out_specs=outs, check_vma=False,
    )
```

time: 874 us -> 268 us (0.31)
  waiting for transfers between devices: 495 us -> 0 us
  Pallas kernels: 0 us -> 244 us
  matrix products: 186 us -> 0 us
  blocking collectives: 64.2 us -> 0 us
  local copies, waits for them, and re-layouts: 60.3 us -> 13 us
  other arithmetic: 46.6 us -> 9.67 us
  between operations: 14.7 us -> 0.71 us
    all_gather x4 -> x0, waiting for transfers between devices: 245 us -> none  [the longest x1 63.7 us: per_device(): branch_rows = lax.all_gather(branch_low, 'head', axis=0, tiled=True)]
    pallas_call x0 -> x1, Pallas kernels: none -> 244 us  [per_device(): pl.pallas_call(lambda *refs: layer_kernel(n_batch, n_head, *refs), out_sh...]
    dot_general x102 -> x0, matrix products: 186 us -> none  [the longest x6 23.8 us: back_dot(): lax.dot_general(left, right, (((1,), (1,)), ((), ())), preferred_element_...]
    reduce_scatter x4 -> x0, waiting for transfers between devices: 176 us -> none  [the longest x1 59 us: per_device(): lax.psum_scatter(jnp.dot(up_act, down_weight, preferred_element_type=jnp....]
    psum x1 -> x0, waiting for transfers between devices: 73 us -> none  [per_device(): lax.psum((query_weight_grad, query_bias_grad, key_weight_grad, value_weig...]
    psum x2 -> x0, blocking collectives: 64.2 us -> none  [the longest x1 42 us: per_device(): lax.psum((first_gain_grad, first_shift_grad, out_bias_grad, second_gain_g...]
    reduce_sum x16 -> x0, other arithmetic: 22.9 us -> none  [the longest x1 5.28 us: per_device(): out_bias_grad = jnp.sum(branch_low.astype(jnp.float32), axis=0)]
    unnamed x124 -> x10, local copies, waits for them, and re-layouts: 16.4 us -> 3.68 us
  transfers between devices with their start and end apart: 9 -> 0, of which waited for: 9 -> 0; matrix products, arithmetic and copies ran while one was open for 6% -> 0% of each run, Pallas kernels for 0% -> 0%
where the time goes in v1:
time: 268 us; the launch traced here: 267 us
  Pallas kernels  244 us (91%)
  local copies, waits for them, and re-layouts  13 us (5%)
  other arithmetic  9.67 us (4%)
    pallas_call x1, Pallas kernels, per_device(): pl.pallas_call(lambda *refs: layer_kernel(n_batch, n_head, *refs), out_sh...  244 us

profile of v1, /device:TPU:1, one launch (start us, length us, event | category | flops | bytes accessed | tf_op | source)
XLA Modules:
  0.0 267.1 jit_solution(3716100412197432856)
XLA Ops:
  0.7 0.7 stack.77
  1.3 0.7 stack.78
  2.0 0.7 stack.70
  2.7 0.7 stack.71
  3.3 0.7 stack.72
  4.0 0.7 stack.73
  4.7 0.7 stack.74
  5.4 0.7 reshape.72
  6.1 0.7 stack.75
  6.8 0.7 copy.41
  7.5 0.7 copy.42
  8.2 0.1 dynamic_update_slice.8
  8.3 0.2 dynamic_update_slice.9
  8.6 0.6 pad.10.refs_8_
  9.2 0.6 pad_convert_fusion.refs_9_
  9.8 2.4 pad_maximum_fusion.refs_5_
  12.2 243.7 %shard_map.357 = (bf16[512,768]{1,0:T(8,128)(2,1)}, bf16[512,768]{1,0:T(8,128)(2,1)}, bf16[3,192,768]{2,1,0:T(8,128)(2,1)}, bf16[1,192,768]{2,1,0:T(8,128)(2,1)}...) custom-call(s32[4]{0:T(128)} %refs_0_.1, s32[4]{0:T(128)} %refs_1_.1, bf16[512,768]{1,0:T(8,128)(2,1)} %refs_2_.1, ...), custom_call_target="tpu_custom_call" | custom-call | tf_op jit(solution)/shard_map/pallas_call | solution.py:824
  255.9 1.7 fusion
  257.6 0.6 constant_dynamic-slice_fusion
  258.3 0.6 reshape.68
  258.9 0.6 reshape.69
  259.5 0.0 copy-start
  259.5 2.8 %convert_bitcast_fusion = (f32[768,192]{0,1:T(8,128)}, f32[768,192]{0,1:T(8,128)}, f32[768,192]{0,1:T(8,128)}, f32[192,768]{1,0:T(8,128)}) fusion(bf16[3,192,768]{2,1,0:T(8,128)(2,1)} %get-tuple-element.28, bf16[1,192,768]{2,1,0:T(8,128)(2,1)} %get-tuple-element.29), kind=kLoop, calls=%fused_computation.3 | loop fusion | flops 589824 | bytes 3538944 | tf_op jit(solution)/shard_map/convert_element_type | solution.py:871
  262.3 0.0 copy-done
  262.3 0.0 copy-start.2
  262.3 2.5 bitcast_convert_fusion
  264.8 0.0 copy-start.1
  264.8 0.0 copy-done.2
  264.8 0.9 copy.48
  265.7 0.5 copy-done.1
  266.2 0.9 copy.49
  (4 shorter events, 0.1 us)
Async XLA Ops:
  259.5 2.8 %copy-start = (bf16[2,768,768]{2,1,0:T(8,128)(2,1)S(1)}, bf16[2,768,768]{2,1,0:T(8,128)(2,1)}, u32[]{:S(2)}) copy-start(bf16[2,768,768]{2,1,0:T(8,128)(2,1)} %get-tuple-element.30) | copy-start | bytes 7077892
  262.3 2.6 copy-start.2
  264.8 1.4 copy-start.1

commit v2 on v1

--- a/solution.py
+++ b/solution.py
@@ -12,7 +12,7 @@
 EPS = 1e-05
 ROOT = math.sqrt(2.0 / math.pi)
 CUBE = 0.044715
-ROW_TILE = 32
+ROW_TILE = 128
 
 
 def mm(left, right):
@@ -53,8 +53,8 @@
     return jnp.sum(value, axis=0, keepdims=True)
 
 
-ATT, OUT, MLP = 0, 1, 2
-KINDS = (ATT, OUT, MLP)
+ATT, OUT, UP, DOWN = range(4)
+KINDS = (ATT, OUT, UP, DOWN)
 MESH = pl.DeviceIdType.MESH
 SUB = 8
 
@@ -85,7 +85,7 @@
             self.extra.append(b + step - 2 * step * bit)
             step *= 2
         self.half_width = wm.shape[-1] // 2
-        self.rows = (wa.shape[1] // n_head, wa.shape[1] // n_head, wm.shape[2])
+        self.rows = (wa.shape[1] // n_head,) * 2 + (wm.shape[2],) * 2
         self.pending = []
 
     def barrier(self):
@@ -104,8 +104,8 @@
 
     def view(self, kind, k, start, count, cols):
         g = self.group(k) if k else self.h
-        if kind == MLP:
-            return self.wm.at[g, :, pl.ds(pl.multiple_of(start, 16), count), cols]
+        if kind >= UP:
+            return self.wm.at[g, pl.ds(kind - UP, 1), pl.ds(pl.multiple_of(start, 16), count), cols]
         first, many = (0, 3) if kind == ATT else (3, 1)
         offset = pl.multiple_of(g * self.rows[kind] + start, 16)
         return self.wa.at[pl.ds(first, many), pl.ds(offset, count), cols]
@@ -120,13 +120,12 @@
             device_id=peer, device_id_type=MESH,
         )
 
-    def gather_start(self, kind):
+    def gather_start(self, kind, k):
         own = self.part(kind, 0, 4, self.quarter, self.cols(self.core))
-        for j in range(self.n_head - 1, 0, -1):
-            self.copy(
-                own, own, self.ag_s.at[kind, j, 0], self.ag_r.at[kind, self.n_head - j, 0],
-                (self.b, self.group(j)),
-            ).start()
+        j = self.n_head - k
+        self.copy(
+            own, own, self.ag_s.at[kind, j, 0], self.ag_r.at[kind, k, 0], (self.b, self.group(j))
+        ).start()
 
     def gather_step(self, kind, k, stage, receive=False):
         mine = self.cols(self.core)
@@ -290,55 +289,87 @@
         own = aux.at[self.group(k)]
         self.copy(own, own, self.ax_s.at[k], self.ax_r.at[k], (self.b, self.group(k))).wait_recv()
 
-    def small_sum(self, small, got, all_heads):
-        for e, peer in enumerate([self.mate, self.near, self.far] + self.extra):
-            copy = self.copy(small, got.at[e], self.sm_s.at[e], self.sm_r.at[e], (peer, self.h))
-            copy.start()
-            copy.wait()
-            small[...] = small[...] + got[e]
-        first = 3 + len(self.extra)
-        copies = []
-        for j in range(1, self.n_head):
-            copy = self.copy(
-                small, all_heads.at[self.h], self.sm_s.at[first + j],
-                self.sm_r.at[first + j], (self.b, self.group(j)),
-            )
-            copy.start()
-            copies.append(copy)
-        all_heads[self.h] = small[...]
-        for copy in copies:
-            copy.wait()
-        total = all_heads[0]
-        for g in range(1, self.n_head):
-            total = total + all_heads[g]
-        small[...] = total
-
-
-def schedule(n_head, gp, rp, fp):
-    others = range(1, n_head)
-    forward = {
-        0: [(gp, OUT, k, 1) for k in others] + [(gp, MLP, 1, 1)],
-        1: [(gp, OUT, k, 2) for k in others] + [(gp, MLP, 1, 2)],
-        2: [(gp, OUT, k, 3) for k in others] + [(gp, MLP, 2, 1)],
-        3: [(gp, MLP, 1, 3), (gp, MLP, 2, 2), (gp, MLP, 3, 1)],
-        4: [(gp, MLP, 2, 3), (gp, MLP, 3, 2)],
-        5: [(gp, MLP, 3, 3)],
-    }
-    units = {
-        1: [(rp, MLP, 0, 1)],
-        2: [(rp, MLP, 0, 2), (rp, MLP, 1, 1)],
-        3: [(rp, MLP, 0, 3), (rp, MLP, 1, 2)],
-    }
-    backward = {
-        0: [(rp, MLP, 2, 1), (rp, MLP, 1, 3)],
-        1: [(rp, MLP, 2, 2), (rp, MLP, 3, 1)],
-        2: [(rp, MLP, 2, 3)] + [(rp, OUT, k, 1) for k in range(n_head)],
-        3: [(rp, MLP, 3, 2)] + [(rp, OUT, k, 2) for k in range(n_head)],
-        4: [(rp, MLP, 3, 3)] + [(rp, OUT, k, 3) for k in range(n_head)],
-        5: [(fp, MLP, 0), (fp, OUT, 0), (fp, MLP, 1), (fp, OUT, 1), (fp, MLP, 2), (fp, OUT, 2)],
-    }
-    return forward, units, backward
-
+    def small_step(self, small, got, all_heads, stage, j=0):
+        peers = [self.mate, self.near, self.far]
+        if stage < 3:
+            src, dst, peer, at = small, got.at[stage], (peers[stage], self.h), stage
+        else:
+            src, dst, peer, at = small, all_heads.at[self.h], (self.b, self.group(j)), 2 + j
+        return self.copy(src, dst, self.sm_s.at[at], self.sm_r.at[at], peer)
+
+    def small_pass(self, small, got, all_heads, stage):
+        if stage == 0:
+            self.small_step(small, got, all_heads, 0).start()
+        elif stage <= 3:
+            self.small_step(small, got, all_heads, stage - 1).wait()
+            small[...] = small[...] + got[stage - 1]
+            if stage < 3:
+                self.small_step(small, got, all_heads, stage).start()
+                return
+            first = 2 + self.n_head
+            for e, peer in enumerate(self.extra):
+                copy = self.copy(
+                    small, got.at[3 + e], self.sm_s.at[first + e], self.sm_r.at[first + e],
+                    (peer, self.h),
+                )
+                copy.start()
+                copy.wait()
+                small[...] = small[...] + got[3 + e]
+            for j in range(1, self.n_head):
+                self.small_step(small, got, all_heads, 3, j).start()
+            all_heads[self.h] = small[...]
+        else:
+            for j in range(1, self.n_head):
+                self.small_step(small, got, all_heads, 3, j).wait()
+            total = all_heads[0]
+            for g in range(1, self.n_head):
+                total = total + all_heads[g]
+            small[...] = total
+
+
+SCHEDULE = {
+    "needA": (("g", 0, 1, 1), ("g", 0, 1, 2), ("g", 0, 2, 1), ("g", 0, 3, 1), ("g", 0, 1, 3), ("g", 1, 1, 1), ("g", 0, 2, 2), ("g", 1, 2, 1), ("g", 0, 1, 4), ("g", 0, 3, 2), ("g", 1, 3, 1), ("g", 1, 1, 2), ("g", 0, 2, 3), ("g", 1, 2, 2), ("g", 2, 1, 1), ("g", 0, 2, 4), ("g", 0, 3, 3), ("g", 1, 3, 2), ("g", 1, 1, 3), ("g", 0, 3, 4),),
+    ("proj", 0): (("g", 1, 2, 3),),
+    ("proj", 1): (("g", 3, 1, 1),),
+    ("proj", 2): (("g", 2, 1, 2),),
+    "maps": (("g", 1, 3, 3),),
+    ("fwd", 1): (("g", 3, 1, 2),),
+    ("fwd", 2): (("g", 2, 2, 1),),
+    ("fwd", 4): (("g", 2, 1, 3),),
+    ("fwd", 5): (("g", 3, 2, 1),),
+    "needO": (("g", 1, 1, 4), ("g", 1, 2, 4), ("g", 1, 3, 4),),
+    "ln2": (("g", 3, 1, 3),),
+    ("mlp0", 0): (("g", 2, 2, 2),),
+    ("mlp1", 0): (("g", 2, 3, 1), ("g", 3, 2, 2),),
+    ("mlpU", 0): (("g", 3, 3, 1),),
+    ("needU", 1): (("g", 2, 1, 4),),
+    ("mlp0", 1): (("g", 2, 2, 3),),
+    ("needD", 1): (("g", 3, 1, 4),),
+    ("mlp1", 1): (("g", 2, 3, 2),),
+    ("mlpD", 1): (("g", 3, 2, 3),),
+    ("needU", 2): (("g", 2, 2, 4),),
+    ("mlp0", 2): (("g", 3, 3, 2), ("r", 3, 0, 1), ("r", 2, 0, 1),),
+    ("needD", 2): (("r", 3, 1, 1), ("g", 3, 2, 4),),
+    ("mlp1", 2): (("g", 2, 3, 3), ("r", 2, 1, 1),),
+    ("mlpU", 2): (("g", 3, 3, 3),),
+    ("needU", 3): (("g", 2, 3, 4),),
+    ("needD", 3): (("r", 3, 2, 1), ("r", 3, 0, 2), ("r", 2, 2, 1), ("g", 3, 3, 4),),
+    ("mlp2", 3): (("r", 2, 0, 2),),
+    "sb": (("r", 3, 1, 2),),
+    "gctx": (("r", 3, 3, 1), ("r", 2, 3, 1),),
+    ("bwd0", 0): (("r", 2, 1, 2),),
+    ("bwd1", 0): (("r", 1, 0, 1), ("r", 1, 1, 1), ("r", 1, 2, 1), ("r", 1, 3, 1),),
+    ("bwd0", 1): (("r", 3, 2, 2),),
+    ("bwd1", 1): (("r", 3, 0, 3),),
+    ("bwd0", 3): (("r", 2, 2, 2),),
+    ("bwd1", 3): (("r", 2, 0, 3),),
+    ("bwd0", 4): (("r", 3, 1, 3),),
+    ("bwd1", 5): (("r", 3, 3, 2),),
+    "dx": (("r", 2, 3, 2), ("r", 2, 1, 3),),
+    "dwa": (("r", 1, 0, 2), ("r", 1, 1, 2), ("r", 1, 2, 2), ("r", 1, 3, 2),),
+    "fb": (("r", 3, 2, 3),),
+    "tail": (("r", 0, 0, 1), ("r", 0, 1, 1), ("r", 2, 2, 3), ("r", 0, 2, 1), ("r", 0, 3, 1), ("s", 1), ("r", 3, 3, 3), ("r", 2, 3, 3), ("r", 1, 0, 3), ("r", 1, 1, 3), ("r", 1, 2, 3), ("r", 1, 3, 3), ("r", 0, 0, 2), ("r", 0, 1, 2), ("r", 0, 2, 2), ("r", 0, 3, 2), ("f", 3, 0), ("s", 2), ("r", 0, 0, 3), ("r", 0, 1, 3), ("r", 0, 2, 3), ("f", 2, 0), ("r", 0, 3, 3), ("f", 3, 1), ("f", 1, 0), ("s", 3), ("f", 2, 1), ("f", 3, 2), ("f", 1, 1), ("f", 3, 3), ("f", 2, 2), ("f", 1, 2), ("f", 0, 0), ("f", 2, 3), ("f", 1, 3), ("f", 0, 1), ("s", 4), ("f", 0, 2), ("f", 0, 3),),
+}
 
 def layer_kernel(
     n_batch, n_head,
@@ -370,6 +401,7 @@
         copy.start()
         return copy
 
+    others = range(1, n_head)
     net = Exchange(n_batch, n_head, wa, wm, recv, fin, more, links)
     att_copies = [load(att_in, wa.at[:, pl.ds(pl.multiple_of(me * gcols, 16), gcols), :], 5)]
     aux_own = load(aux_in, aux.at[me], 3)
@@ -383,14 +415,40 @@
     net.barrier()
     for copy in att_copies:
         copy.wait()
-    net.gather_start(ATT)
+    for k in others:
+        net.gather_start(ATT, k)
     aux_own.wait()
     for j in range(1, n_head):
         net.aux_copy(aux, j).start()
-    net.gather_start(OUT)
+    for k in others:
+        net.gather_start(OUT, k)
     for copy in mlp_copies:
         copy.wait()
-    net.gather_start(MLP)
+    for k in others:
+        net.gather_start(UP, k)
+        net.gather_start(DOWN, k)
+
+    def event(op, first, *rest):
+        if op == "g":
+            net.gather_pass(first, *rest)
+        elif op == "r":
+            net.reduce_pass(first, *rest)
+        elif op == "f":
+            net.final_pass(first, *rest)
+        else:
+            net.small_pass(small, got, all_heads, first)
+
+    def take(slot):
+        for item in SCHEDULE.get(slot, ()):
+            event(*item)
+
+    def take_at(index, count, slot):
+        for value in range(count):
+            if (slot, value) in SCHEDULE:
+                @pl.when(index == value)
+                def _():
+                    take((slot, value))
+
 
     flag = flags[me].astype(F32)
     bound = bounds[me]
@@ -422,10 +480,9 @@
         return state
 
     each_tile(first_norm)
-    for stage in (1, 2, 3, 4):
-        for k in range(1, n_head):
-            net.gather_pass(ATT, k, stage)
-    for k in range(1, n_head):
+    take("ln1")
+    take("needA")
+    for k in others:
         net.aux_wait(aux, k)
 
     tile_n = 256
@@ -445,6 +502,7 @@
                 if bias_row is not None:
                     value = value + bias
                 mem_out[:, cols] = value.astype(BF16)
+        take(("proj", kind))
 
     cwm[...] = jnp.zeros_like(cwm)
     per_group = heads // n_head
@@ -488,18 +546,9 @@
         value = jnp.exp(offset * offset * isp[pl.ds(head, 1), :]) * nrs[pl.ds(head, 1), :]
         return offset, value
 
-    def at(index, slots):
-        for value, events in slots.items():
-            @pl.when(index == value)
-            def _():
-                for event, *rest in events:
-                    event(*rest)
-
-    gp, rp, fp = net.gather_pass, net.reduce_pass, net.final_pass
-    forward_slots, unit_slots, backward_slots = schedule(n_head, gp, rp, fp)
+    take("maps")
 
     def forward_pair(p, state):
-        at(p, forward_slots)
         lanes = pl.ds(pl.multiple_of(p * 2 * head_width, 2 * head_width), 2 * head_width)
         keys = ks[:, lanes]
         vals = vs[:, lanes]
@@ -529,15 +578,17 @@
                     u_s[span, 0 : 2 * head_width] = value
                 else:
                     ctx[span, lanes] = (value + u_s[span, 0 : 2 * head_width]).astype(BF16)
+        take_at(p, pairs, "fwd")
         return state
 
     lax.fori_loop(0, pairs, forward_pair, 0)
 
-    for k in range(1, n_head):
-        gp(OUT, k, 4)
+    take("needO")
 
     for n in range(0, width, tile_n):
         hid[:, n : n + tile_n] = mm(ctx[...], wa[3, :, n : n + tile_n])
+
+    take("out")
 
     def second_norm(span, state):
         hidden = xs[span, :].astype(F32) + (hid[span, :] + nrm[2:3, :])
@@ -549,13 +600,18 @@
         return state
 
     each_tile(second_norm)
+    take("ln2")
 
     def units(k, state):
         g = lax.rem(me + k, n_head)
-        at(k, {i: [(gp, MLP, i, 4)] for i in range(1, n_head)})
+        take_at(k, n_head, "needU")
         for n in range(0, width, tile_n):
             cols = slice(n, n + tile_n)
             u_s[:, cols] = mm(x2[...], wm[g, 0, :, cols])
+        take_at(k, n_head, "mlp0")
+        take_at(k, n_head, "needD")
+        for n in range(0, width, tile_n):
+            cols = slice(n, n + tile_n)
             g_s[:, cols] = mm_nt(gos[...], wm[g, 1, cols, :])
         bias = aux[g, 2:3, :]
 
@@ -571,18 +627,32 @@
             return total + fold8(low.astype(F32))
 
         total = each_tile(activate, zero_sum)
-        at(k, unit_slots)
+        take_at(k, n_head, "mlp1")
         small[pl.ds(8 + g, 1), :] = row_sum(total)
         for n in range(0, width, tile_n):
             cols = slice(n, n + tile_n)
             acc[:, cols] += mm(act_s[...], wm[g, 1, :, cols])
             dx2[:, cols] += mm_nt(du_s[...], wm[g, 0, cols, :])
-        at(k, {i: [(net.gather_sent, MLP, i)] for i in range(n_head)})
+        take_at(k, n_head, "mlp2")
+
+        def each_group(*calls):
+            for value in range(n_head):
+                @pl.when(k == value)
+                def _():
+                    for call, kind, *rest in calls:
+                        call(kind, value, *rest)
+
+        each_group((net.gather_sent, UP), (net.gather_sent, DOWN))
         for n in range(0, width, tile_n):
             cols = slice(n, n + tile_n)
             wm[g, 1, :, cols] = mm_tn(act_s[...], gos[:, cols]).astype(BF16)
+        each_group((net.reduce_pass, DOWN, 0))
+        take_at(k, n_head, "mlpD")
+        for n in range(0, width, tile_n):
+            cols = slice(n, n + tile_n)
             wm[g, 0, :, cols] = mm_tn(x2[...], du_s[:, cols]).astype(BF16)
-        at(k, {i: [(rp, MLP, i, 0)] for i in range(n_head)})
+        each_group((net.reduce_pass, UP, 0))
+        take_at(k, n_head, "mlpU")
         return state
 
     lax.fori_loop(0, n_head, units, 0)
@@ -614,19 +684,21 @@
     small[4:5, :] = row_sum(sums[1])
     small[2:3, :] = row_sum(sums[2])
     small[5:6, :] = row_sum(sums[3])
+    take("sb")
     for n in range(0, width, tile_n):
         cols = slice(n, n + tile_n)
         gcs[:, cols] = mm_nt(act_s[...], wa[3, cols, :]).astype(BF16)
+    take("gctx")
     for k in range(n_head):
         net.gather_sent(OUT, k)
     for n in range(0, width, tile_n):
         cols = slice(n, n + tile_n)
         wa[3, :, cols] = mm_tn(ctx[...], act_s[:, cols]).astype(BF16)
     for k in range(n_head):
-        rp(OUT, k, 0)
+        net.reduce_pass(OUT, k, 0)
+    take("dwo")
 
     def backward_pair(p, state):
-        at(p, backward_slots)
         lanes = pl.ds(pl.multiple_of(p * 2 * head_width, 2 * head_width), 2 * head_width)
         keys = ks[:, lanes]
         vals = vs[:, lanes]
@@ -689,6 +761,7 @@
             grad_spread = (row_sum(sum2) * inverse - row_sum(sum0)) * (0.5 * inverse)
             pg[one, :] = grad_centre * centre * (1.0 - centre)
             pg[pl.ds(16 + head, 1), :] = 0.02 * grad_spread * wsg[one, :]
+            take_at(p, pairs, ("bwd0", "bwd1")[e])
         return state
 
     lax.fori_loop(0, pairs, backward_pair, 0)
@@ -713,6 +786,8 @@
             slopes[0], high
         )
         act_s[:, cols] = (dqs[:, cols] * scale + value).astype(BF16)
+    take("mem")
+
     def bias_sums(span, sums):
         return (
             sums[0] + fold8(act_s[span, :].astype(F32)),
@@ -722,6 +797,7 @@
     sums = each_tile(bias_sums, (zero_sum,) * 2)
     small[6:7, :] = row_sum(sums[0])
     small[7:8, :] = row_sum(sums[1]) + row_sum(gmv[...].astype(F32))
+    take("bias")
 
     for n in range(0, width, tile_n):
         cols = slice(n, n + tile_n)
@@ -730,6 +806,7 @@
             + mm(dks[...], wa[1, :, cols])
             + mm(dvs[...], wa[2, :, cols])
         )
+    take("dx")
     for k in range(n_head):
         net.gather_sent(ATT, k)
     for n in range(0, width, tile_n):
@@ -743,9 +820,8 @@
         ).astype(BF16)
 
     for k in range(n_head):
-        rp(ATT, k, 0)
-    for k in range(n_head):
-        rp(ATT, k, 1)
+        net.reduce_pass(ATT, k, 0)
+    take("dwa")
 
     def first_back(span, sums):
         normed, factor = norm_rows(xs[span, :].astype(F32))
@@ -760,20 +836,20 @@
     sums = each_tile(first_back, (zero_sum,) * 2)
     small[0:1, :] = row_sum(sums[0])
     small[1:2, :] = row_sum(sums[1])
+    event("s", 0)
     outs = [load(du_s, dx_out, 0)]
-    for k in range(n_head):
-        rp(ATT, k, 2)
-    net.small_sum(small, got, all_heads)
-    outs += [load(small, small_out, 1)]
-    for k in range(n_head):
-        rp(ATT, k, 3)
-    fp(MLP, 3)
-    outs += [load(fin[MLP], dmlp_out, 2)]
-    fp(OUT, 3)
-    outs += [load(fin[OUT], dout_out, 3)]
-    for stage in range(4):
-        fp(ATT, stage)
-    outs += [load(fin[ATT], dqkv_out, 4)]
+    take("fb")
+    finished = {
+        ("f", ATT, 3): (fin[ATT], dqkv_out, 1),
+        ("f", OUT, 3): (fin[OUT], dout_out, 2),
+        ("f", UP, 3): (fin[UP], dmlp_out.at[pl.ds(0, 1)], 3),
+        ("f", DOWN, 3): (fin[DOWN], dmlp_out.at[pl.ds(1, 1)], 4),
+        ("s", 4): (small, small_out, 5),
+    }
+    for item in SCHEDULE["tail"]:
+        event(*item)
+        if item in finished:
+            outs.append(load(*finished[item]))
     net.all_sent()
     for j in range(1, n_head):
         net.aux_copy(aux, j).wait_send()
@@ -817,7 +893,7 @@
     any_spec = pl.BlockSpec(memory_space=pl.ANY)
     smem = pl.BlockSpec(memory_space=pltpu.SMEM)
     dma = pltpu.SemaphoreType.DMA
-    halves = ((3, gcols), (1, gcols), (2, width))
+    halves = ((3, gcols), (1, gcols), (1, width), (1, width))
     recv = tuple(
         tuple(vm(n_head, t, r // pieces, width // 2) for t, r in halves) for pieces in (1, 2, 4, 4)
     )
@@ -852,8 +928,8 @@
             recv,
             tuple(vm(t, r, width) for t, r in halves),
             tuple(vm(extra, t, r // 4, width // 2) for t, r in halves) if extra else (),
-            (dma((3, n_head, 4)), dma((3, n_head, 4)), dma((3, n_head, 4)), dma((3, n_head, 4)),
-             dma((3, 3)), dma((3, 3)), dma((3, max(extra, 1))), dma((3, max(extra, 1))),
+            (dma((4, n_head, 4)), dma((4, n_head, 4)), dma((4, n_head, 4)), dma((4, n_head, 4)),
+             dma((4, 3)), dma((4, 3)), dma((4, max(extra, 1))), dma((4, max(extra, 1))),
              dma((3 + extra + n_head,)),
              dma((3 + extra + n_head,)), dma((n_head,)), dma((n_head,))),
             dma((8,)),

time: 268 us -> 199 us (0.74)
  Pallas kernels: 244 us -> 174 us
    pallas_call x1, Pallas kernels: 244 us -> 174 us  [per_device(): pl.pallas_call(lambda *refs: layer_kernel(n_batch, n_head, *refs), out_sh...]
where the time goes in v2:
time: 199 us; the launch traced here: 197 us
  Pallas kernels  174 us (87%)
  local copies, waits for them, and re-layouts  13 us (7%)
  other arithmetic  9.67 us (5%)
    pallas_call x1, Pallas kernels, per_device(): pl.pallas_call(lambda *refs: layer_kernel(n_batch, n_head, *refs), out_sh...  174 us
    another operation x7, local copies, waits for them, and re-layouts, per_device(): jnp.stack([first_gain, first_shift, out_bias, second_gain, second_shift,...  4.15 us

profile of v2, /device:TPU:1, one launch (start us, length us, event | category | flops | bytes accessed | tf_op | source)
XLA Modules:
  0.0 197.3 jit_solution(9672166995796956157)
XLA Ops:
  0.7 0.7 stack.77
  1.3 0.7 stack.78
  2.0 0.7 stack.70
  2.7 0.7 stack.71
  3.3 0.7 stack.72
  4.0 0.7 stack.73
  4.7 0.7 stack.74
  5.4 0.7 reshape.72
  6.1 0.7 stack.75
  6.8 0.7 copy.41
  7.5 0.7 copy.42
  8.2 0.1 dynamic_update_slice.8
  8.3 0.2 dynamic_update_slice.9
  8.6 0.6 pad.10.refs_8_
  9.2 0.6 pad_convert_fusion.refs_9_
  9.8 2.4 %pad_maximum_fusion.refs_5_ = bf16[4,192,768]{2,1,0:T(8,128)(2,1)} fusion(bf16[1,192,768]{2,1,0:T(8,128)(2,1)} %bitcast.44, bf16[1,192,768]{2,1,0:T(8,128)(2,1)} %bitcast.45, bf16[1,192,768]{2,1,0:T(8,128)(2,1)} %bitcast.46, bf16[1,192,768]{2,1,0:T(8,128)(2,1)} %bitcast.47), kind=kLoop, calls=%fused_computation | loop fusion | flops 1769472 | bytes 2359296 | tf_op jit(solution)/shard_map/stack | solution.py:872
  12.2 173.9 %shard_map.357 = (bf16[512,768]{1,0:T(8,128)(2,1)}, bf16[512,768]{1,0:T(8,128)(2,1)}, bf16[3,192,768]{2,1,0:T(8,128)(2,1)}, bf16[1,192,768]{2,1,0:T(8,128)(2,1)}...) custom-call(s32[4]{0:T(128)} %refs_0_.1, s32[4]{0:T(128)} %refs_1_.1, bf16[512,768]{1,0:T(8,128)(2,1)} %refs_2_.1, ...), custom_call_target="tpu_custom_call" | custom-call | tf_op jit(solution)/shard_map/pallas_call | solution.py:900
  186.1 1.7 fusion
  187.8 0.6 constant_dynamic-slice_fusion
  188.4 0.6 reshape.68
  189.0 0.6 reshape.69
  189.6 0.0 copy-start
  189.6 2.8 %convert_bitcast_fusion = (f32[768,192]{0,1:T(8,128)}, f32[768,192]{0,1:T(8,128)}, f32[768,192]{0,1:T(8,128)}, f32[192,768]{1,0:T(8,128)}) fusion(bf16[3,192,768]{2,1,0:T(8,128)(2,1)} %get-tuple-element.28, bf16[1,192,768]{2,1,0:T(8,128)(2,1)} %get-tuple-element.29), kind=kLoop, calls=%fused_computation.3 | loop fusion | flops 589824 | bytes 3538944 | tf_op jit(solution)/shard_map/convert_element_type | solution.py:947
  192.4 0.0 copy-done
  192.5 0.0 copy-start.2
  192.5 2.5 %bitcast_convert_fusion = (f32[768,768]{1,0:T(8,128)}, f32[768,768]{1,0:T(8,128)}) fusion(bf16[2,768,768]{2,1,0:T(8,128)(2,1)S(1)} %copy-done), kind=kLoop, calls=%fused_computation.1 | loop fusion | flops 1179648 | bytes 7077888 | tf_op jit(solution)/shard_map/convert_element_type | solution.py:950
  195.0 0.0 copy-start.1
  195.0 0.0 copy-done.2
  195.0 0.9 copy.48
  195.9 0.5 copy-done.1
  196.4 0.9 copy.49
  (4 shorter events, 0.1 us)
Async XLA Ops:
  189.6 2.8 %copy-start = (bf16[2,768,768]{2,1,0:T(8,128)(2,1)S(1)}, bf16[2,768,768]{2,1,0:T(8,128)(2,1)}, u32[]{:S(2)}) copy-start(bf16[2,768,768]{2,1,0:T(8,128)(2,1)} %get-tuple-element.30) | copy-start | bytes 7077892
  192.5 2.6 %copy-start.2 = (bf16[512,768]{1,0:T(8,128)(2,1)S(1)}, bf16[512,768]{1,0:T(8,128)(2,1)}, u32[]{:S(2)}) copy-start(bf16[512,768]{1,0:T(8,128)(2,1)} %get-tuple-element.78) | copy-start | bytes 2359300
  195.0 1.4 copy-start.1

commit v3 on v2

--- a/solution.py
+++ b/solution.py
@@ -55,16 +55,28 @@
 
 ATT, OUT, UP, DOWN = range(4)
 KINDS = (ATT, OUT, UP, DOWN)
+DIRECT = (ATT, OUT)
 MESH = pl.DeviceIdType.MESH
 SUB = 8
 
 
+def nearest_first(place, count):
+    return sorted(range(count), key=lambda other: (abs(other - place), other))
+
+
+def pick(index, values):
+    chosen = values[0]
+    for at, value in enumerate(values[1:], 1):
+        chosen = jnp.where(index == at, value, chosen)
+    return chosen
+
+
 class Exchange:
-    def __init__(self, n_batch, n_head, wa, wm, recv, fin, more, sems):
-        self.n_head = n_head
+    def __init__(self, n_batch, n_head, wa, wm, recv, fin, more, smalls, sems):
+        self.n_head, self.smalls = n_head, smalls
         self.wa, self.wm = wa, wm
         self.recv, self.fin, self.more = recv, fin, more
-        (self.ag_s, self.ag_r, self.rs_s, self.rs_r, self.fin_s, self.fin_r, self.ex_s, self.ex_r,
+        (self.ag_s, self.ag_r, self.ag_o, self.rs_s, self.rs_r, self.fin_s, self.fin_r, self.ex_s, self.ex_r,
          self.sm_s, self.sm_r, self.ax_s, self.ax_r) = sems
         b, h = lax.axis_index("batch"), lax.axis_index("head")
         self.b, self.h = b, h
@@ -84,6 +96,10 @@
             bit = lax.rem(lax.div(b, step), 2)
             self.extra.append(b + step - 2 * step * bit)
             step *= 2
+        orders = [nearest_first(place, n_head) for place in range(n_head)]
+        self.groups = [
+            h if k == 0 else pick(h, [order[k] for order in orders]) for k in range(n_head)
+        ]
         self.half_width = wm.shape[-1] // 2
         self.rows = (wa.shape[1] // n_head,) * 2 + (wm.shape[2],) * 2
         self.pending = []
@@ -91,19 +107,22 @@
     def barrier(self):
         signal = pltpu.get_barrier_semaphore()
         peers = [(p, self.h) for p in [self.mate, self.near, self.far] + self.extra]
-        peers += [(self.b, self.group(k)) for k in range(1, self.n_head)]
+        peers += [(self.b, self.turn(k)) for k in range(1, self.n_head)]
         for peer in peers:
             pl.semaphore_signal(signal, inc=1, device_id=peer, device_id_type=MESH)
         pl.semaphore_wait(signal, len(peers))
 
     def group(self, k):
-        return lax.rem(self.h + k, self.n_head)
+        return self.groups[k]
+
+    def turn(self, j):
+        return lax.rem(self.h + j, self.n_head)
 
     def cols(self, which):
         return pl.ds(pl.multiple_of(which * self.half_width, 128), self.half_width)
 
     def view(self, kind, k, start, count, cols):
-        g = self.group(k) if k else self.h
+        g = self.group(k)
         if kind >= UP:
             return self.wm.at[g, pl.ds(kind - UP, 1), pl.ds(pl.multiple_of(start, 16), count), cols]
         first, many = (0, 3) if kind == ATT else (3, 1)
@@ -120,12 +139,34 @@
             device_id=peer, device_id_type=MESH,
         )
 
-    def gather_start(self, kind, k):
+    def own_sends(self, kind):
         own = self.part(kind, 0, 4, self.quarter, self.cols(self.core))
-        j = self.n_head - k
-        self.copy(
-            own, own, self.ag_s.at[kind, j, 0], self.ag_r.at[kind, k, 0], (self.b, self.group(j))
-        ).start()
+        if kind in DIRECT:
+            targets = [(self.group(k), None) for k in range(1, self.n_head)]
+        else:
+            targets = [(self.h + 1, self.h < self.n_head - 1), (self.h - 1, self.h > 0)]
+        for at, (target, allowed) in enumerate(targets):
+            copy = self.copy(
+                own, own, self.ag_s.at[kind, at, 0], self.ag_r.at[kind, self.h, 0],
+                (self.b, target),
+            )
+            yield copy, allowed
+
+    def gather_start(self, kind):
+        for copy, allowed in self.own_sends(kind):
+            if allowed is None:
+                copy.start()
+            else:
+                pl.when(allowed)(copy.start)
+
+    def onward(self, kind, k):
+        g = self.group(k)
+        ref = self.part(kind, k, 4, self.quarter, self.cols(self.core))
+        target = jnp.where(g < self.h, self.h + 1, self.h - 1)
+        copy = self.copy(
+            ref, ref, self.ag_o.at[kind, k], self.ag_r.at[kind, g, 0], (self.b, target)
+        )
+        return copy, (target >= 0) & (target < self.n_head)
 
     def gather_step(self, kind, k, stage, receive=False):
         mine = self.cols(self.core)
@@ -142,28 +183,34 @@
         else:
             ref = self.part(kind, k, 1, 0, self.cols(1 - self.core) if receive else mine)
             peer = (self.mate, self.h)
+        at = self.group(k) if stage == 0 else k
         return self.copy(
-            ref, ref, self.ag_s.at[kind, k, stage], self.ag_r.at[kind, k, stage], peer
+            ref, ref, self.ag_s.at[kind, k, stage], self.ag_r.at[kind, at, stage], peer
         )
 
     def gather_pass(self, kind, k, stage):
         self.gather_step(kind, k, stage - 1, receive=True).wait_recv()
+        if stage == 1 and kind not in DIRECT:
+            copy, allowed = self.onward(kind, k)
+            pl.when(allowed)(copy.start)
         if stage < 4:
             self.gather_step(kind, k, stage).start()
 
     def gather_sent(self, kind, k):
         if k == 0:
-            own = self.part(kind, 0, 4, self.quarter, self.cols(self.core))
-            for j in range(1, self.n_head):
-                self.copy(
-                    own, own, self.ag_s.at[kind, j, 0], self.ag_r.at[kind, j, 0],
-                    (self.b, self.group(j)),
-                ).wait_send()
-        else:
-            for stage in (1, 2, 3):
-                self.gather_step(kind, k, stage).wait_send()
-
-    def reduce_step(self, kind, k, stage):
+            for copy, allowed in self.own_sends(kind):
+                if allowed is None:
+                    copy.wait_send()
+                else:
+                    pl.when(allowed)(copy.wait_send)
+            return
+        for stage in (1, 2, 3):
+            self.gather_step(kind, k, stage).wait_send()
+        if kind not in DIRECT:
+            copy, allowed = self.onward(kind, k)
+            pl.when(allowed)(copy.wait_send)
+
+    def reduce_step(self, kind, k, stage, receive=False):
         mine = self.cols(self.core)
         if stage == 0:
             src, peer = self.part(kind, k, 1, 0, self.cols(1 - self.core)), (self.mate, self.h)
@@ -173,9 +220,12 @@
             src, peer = self.part(kind, k, 4, self.other_quarter, mine), (self.near, self.h)
         else:
             src, peer = self.part(kind, k, 4, self.quarter, mine), (self.b, self.group(k))
+        at = k
+        if stage == 3 and not receive:
+            at = lax.rem(self.h - self.group(k) + self.n_head, self.n_head)
         return self.copy(
-            src, self.recv[stage][kind].at[k], self.rs_s.at[kind, k, stage],
-            self.rs_r.at[kind, k, stage], peer,
+            src, self.recv[stage][kind].at[at], self.rs_s.at[kind, k, stage],
+            self.rs_r.at[kind, at, stage], peer,
         )
 
     def add_rows(self, kind, k, start, count, received, out=None):
@@ -184,11 +234,14 @@
         target = own if out is None else out
         sources = [buf.at[k, :, pl.ds(pl.multiple_of(start - base, 16), count), :] for buf, base in received]
         kinds = own.shape[0]
-        tile = 48
+        tile = min(count, 192)
 
         for t in range(kinds):
             def step(i, state):
                 span = pl.ds(pl.multiple_of(i * tile, 16), tile)
+                if len(sources) == 1:
+                    target[t, span, :] = own[t, span, :] + sources[0][t, span, :]
+                    return state
                 total = own[t, span, :].astype(F32)
                 for source in sources:
                     total = total + source[t, span, :].astype(F32)
@@ -238,13 +291,13 @@
     def final_pass(self, kind, stage):
         if stage == 0:
             for k in range(1, self.n_head):
-                self.reduce_step(kind, k, 3).wait_recv()
+                self.reduce_step(kind, k, 3, receive=True).wait_recv()
             quarter = self.rows[kind] // 4
             last = self.recv[3][kind]
             mine = self.cols(self.core)
             own = self.view(kind, 0, self.quarter * quarter, quarter, mine)
             target = self.fin_part(kind, 4, self.quarter, mine)
-            tile = 48
+            tile = min(quarter, 192)
             for t in range(own.shape[0]):
                 def step(i, state):
                     span = pl.ds(pl.multiple_of(i * tile, 16), tile)
@@ -282,104 +335,101 @@
     def aux_copy(self, aux, j):
         own = aux.at[self.h]
         return self.copy(
-            own, own, self.ax_s.at[j], self.ax_r.at[self.n_head - j], (self.b, self.group(j))
+            own, own, self.ax_s.at[j], self.ax_r.at[self.n_head - j], (self.b, self.turn(j))
         )
 
     def aux_wait(self, aux, k):
-        own = aux.at[self.group(k)]
-        self.copy(own, own, self.ax_s.at[k], self.ax_r.at[k], (self.b, self.group(k))).wait_recv()
-
-    def small_step(self, small, got, all_heads, stage, j=0):
+        own = aux.at[self.turn(k)]
+        self.copy(own, own, self.ax_s.at[k], self.ax_r.at[k], (self.b, self.turn(k))).wait_recv()
+
+    def small_step(self, which, stage, j=0):
+        value, got, all_heads = self.smalls[which]
         peers = [self.mate, self.near, self.far]
         if stage < 3:
-            src, dst, peer, at = small, got.at[stage], (peers[stage], self.h), stage
+            src, dst, peer, at = value, got.at[stage], (peers[stage], self.h), stage
         else:
-            src, dst, peer, at = small, all_heads.at[self.h], (self.b, self.group(j)), 2 + j
-        return self.copy(src, dst, self.sm_s.at[at], self.sm_r.at[at], peer)
-
-    def small_pass(self, small, got, all_heads, stage):
+            src, dst, peer, at = value, all_heads.at[self.h], (self.b, self.turn(j)), 2 + j
+        return self.copy(src, dst, self.sm_s.at[which, at], self.sm_r.at[which, at], peer)
+
+    def small_pass(self, which, stage):
+        value, got, all_heads = self.smalls[which]
         if stage == 0:
-            self.small_step(small, got, all_heads, 0).start()
+            self.small_step(which, 0).start()
         elif stage <= 3:
-            self.small_step(small, got, all_heads, stage - 1).wait()
-            small[...] = small[...] + got[stage - 1]
+            self.small_step(which, stage - 1).wait()
+            value[...] = value[...] + got[stage - 1]
             if stage < 3:
-                self.small_step(small, got, all_heads, stage).start()
+                self.small_step(which, stage).start()
                 return
             first = 2 + self.n_head
             for e, peer in enumerate(self.extra):
                 copy = self.copy(
-                    small, got.at[3 + e], self.sm_s.at[first + e], self.sm_r.at[first + e],
-                    (peer, self.h),
+                    value, got.at[3 + e], self.sm_s.at[which, first + e],
+                    self.sm_r.at[which, first + e], (peer, self.h),
                 )
                 copy.start()
                 copy.wait()
-                small[...] = small[...] + got[3 + e]
+                value[...] = value[...] + got[3 + e]
             for j in range(1, self.n_head):
-                self.small_step(small, got, all_heads, 3, j).start()
-            all_heads[self.h] = small[...]
+                self.small_step(which, 3, j).start()
+            all_heads[self.h] = value[...]
         else:
             for j in range(1, self.n_head):
-                self.small_step(small, got, all_heads, 3, j).wait()
+                self.small_step(which, 3, j).wait()
             total = all_heads[0]
             for g in range(1, self.n_head):
                 total = total + all_heads[g]
-            small[...] = total
+            value[...] = total
 
 
 SCHEDULE = {
-    "needA": (("g", 0, 1, 1), ("g", 0, 1, 2), ("g", 0, 2, 1), ("g", 0, 3, 1), ("g", 0, 1, 3), ("g", 1, 1, 1), ("g", 0, 2, 2), ("g", 1, 2, 1), ("g", 0, 1, 4), ("g", 0, 3, 2), ("g", 1, 3, 1), ("g", 1, 1, 2), ("g", 0, 2, 3), ("g", 1, 2, 2), ("g", 2, 1, 1), ("g", 0, 2, 4), ("g", 0, 3, 3), ("g", 1, 3, 2), ("g", 1, 1, 3), ("g", 0, 3, 4),),
-    ("proj", 0): (("g", 1, 2, 3),),
-    ("proj", 1): (("g", 3, 1, 1),),
-    ("proj", 2): (("g", 2, 1, 2),),
-    "maps": (("g", 1, 3, 3),),
-    ("fwd", 1): (("g", 3, 1, 2),),
-    ("fwd", 2): (("g", 2, 2, 1),),
-    ("fwd", 4): (("g", 2, 1, 3),),
-    ("fwd", 5): (("g", 3, 2, 1),),
+    "needA": (("g", 0, 1, 1), ("g", 0, 1, 2), ("g", 0, 2, 1), ("g", 1, 1, 1), ("g", 0, 3, 1), ("g", 1, 2, 1), ("g", 0, 1, 3), ("g", 0, 2, 2), ("g", 1, 1, 2), ("g", 0, 1, 4), ("g", 1, 3, 1), ("g", 0, 3, 2), ("g", 1, 2, 2), ("g", 2, 1, 1), ("g", 0, 2, 3), ("g", 1, 3, 2), ("g", 1, 1, 3), ("g", 0, 2, 4), ("g", 3, 1, 1), ("g", 2, 2, 1), ("g", 0, 3, 3), ("g", 2, 1, 2), ("g", 1, 2, 3), ("g", 0, 3, 4),),
+    ("proj", 0): (("g", 3, 2, 1),),
+    ("proj", 1): (("g", 1, 3, 3), ("g", 3, 1, 2),),
+    ("fwd", 0): (("g", 2, 2, 2), ("g", 2, 3, 1),),
+    ("fwd", 3): (("g", 2, 1, 3), ("g", 3, 2, 2), ("g", 3, 3, 1),),
+    ("fwd", 5): (("g", 2, 3, 2),),
     "needO": (("g", 1, 1, 4), ("g", 1, 2, 4), ("g", 1, 3, 4),),
-    "ln2": (("g", 3, 1, 3),),
-    ("mlp0", 0): (("g", 2, 2, 2),),
-    ("mlp1", 0): (("g", 2, 3, 1), ("g", 3, 2, 2),),
-    ("mlpU", 0): (("g", 3, 3, 1),),
+    ("mlp0", 0): (("g", 3, 1, 3), ("g", 3, 3, 2),),
+    ("mlp2", 0): (("g", 2, 2, 3),),
     ("needU", 1): (("g", 2, 1, 4),),
-    ("mlp0", 1): (("g", 2, 2, 3),),
+    ("mlp0", 1): (("g", 3, 2, 3), ("r", 3, 0, 1),),
     ("needD", 1): (("g", 3, 1, 4),),
-    ("mlp1", 1): (("g", 2, 3, 2),),
-    ("mlpD", 1): (("g", 3, 2, 3),),
+    ("mlp1", 1): (("g", 2, 3, 3), ("r", 2, 0, 1),),
+    ("mlpU", 1): (("g", 3, 3, 3),),
     ("needU", 2): (("g", 2, 2, 4),),
-    ("mlp0", 2): (("g", 3, 3, 2), ("r", 3, 0, 1), ("r", 2, 0, 1),),
-    ("needD", 2): (("r", 3, 1, 1), ("g", 3, 2, 4),),
-    ("mlp1", 2): (("g", 2, 3, 3), ("r", 2, 1, 1),),
-    ("mlpU", 2): (("g", 3, 3, 3),),
+    ("mlp0", 2): (("r", 3, 1, 1), ("r", 2, 1, 1),),
+    ("needD", 2): (("g", 3, 2, 4),),
+    ("mlp1", 2): (("r", 3, 0, 2),),
+    ("mlp2", 2): (("r", 2, 0, 2),),
     ("needU", 3): (("g", 2, 3, 4),),
-    ("needD", 3): (("r", 3, 2, 1), ("r", 3, 0, 2), ("r", 2, 2, 1), ("g", 3, 3, 4),),
-    ("mlp2", 3): (("r", 2, 0, 2),),
-    "sb": (("r", 3, 1, 2),),
-    "gctx": (("r", 3, 3, 1), ("r", 2, 3, 1),),
-    ("bwd0", 0): (("r", 2, 1, 2),),
-    ("bwd1", 0): (("r", 1, 0, 1), ("r", 1, 1, 1), ("r", 1, 2, 1), ("r", 1, 3, 1),),
-    ("bwd0", 1): (("r", 3, 2, 2),),
-    ("bwd1", 1): (("r", 3, 0, 3),),
-    ("bwd0", 3): (("r", 2, 2, 2),),
-    ("bwd1", 3): (("r", 2, 0, 3),),
-    ("bwd0", 4): (("r", 3, 1, 3),),
-    ("bwd1", 5): (("r", 3, 3, 2),),
-    "dx": (("r", 2, 3, 2), ("r", 2, 1, 3),),
-    "dwa": (("r", 1, 0, 2), ("r", 1, 1, 2), ("r", 1, 2, 2), ("r", 1, 3, 2),),
-    "fb": (("r", 3, 2, 3),),
-    "tail": (("r", 0, 0, 1), ("r", 0, 1, 1), ("r", 2, 2, 3), ("r", 0, 2, 1), ("r", 0, 3, 1), ("s", 1), ("r", 3, 3, 3), ("r", 2, 3, 3), ("r", 1, 0, 3), ("r", 1, 1, 3), ("r", 1, 2, 3), ("r", 1, 3, 3), ("r", 0, 0, 2), ("r", 0, 1, 2), ("r", 0, 2, 2), ("r", 0, 3, 2), ("f", 3, 0), ("s", 2), ("r", 0, 0, 3), ("r", 0, 1, 3), ("r", 0, 2, 3), ("f", 2, 0), ("r", 0, 3, 3), ("f", 3, 1), ("f", 1, 0), ("s", 3), ("f", 2, 1), ("f", 3, 2), ("f", 1, 1), ("f", 3, 3), ("f", 2, 2), ("f", 1, 2), ("f", 0, 0), ("f", 2, 3), ("f", 1, 3), ("f", 0, 1), ("s", 4), ("f", 0, 2), ("f", 0, 3),),
+    ("mlp0", 3): (("r", 3, 2, 1), ("r", 2, 2, 1), ("r", 3, 0, 3),),
+    ("needD", 3): (("g", 3, 3, 4),),
+    ("mlp2", 3): (("r", 3, 1, 2), ("r", 2, 0, 3),),
+    ("mlpU", 3): (("r", 2, 1, 2),),
+    "sb": (("r", 3, 3, 1), ("r", 2, 3, 1),),
+    "gctx": (("r", 3, 1, 3), ("s", 0, 1),),
+    ("bwd0", 0): (("r", 3, 2, 2), ("r", 2, 1, 3), ("s", 0, 2), ("r", 1, 0, 1), ("r", 1, 1, 1), ("r", 1, 2, 1), ("r", 1, 3, 1),),
+    ("bwd0", 2): (("r", 3, 2, 3), ("r", 2, 2, 2),),
+    ("bwd1", 3): (("r", 3, 3, 2),),
+    ("bwd1", 4): (("r", 2, 2, 3),),
+    "mem": (("s", 0, 3), ("r", 1, 0, 2), ("r", 3, 3, 3), ("r", 1, 1, 2), ("r", 2, 3, 2),),
+    "bias": (("r", 1, 2, 2),),
+    "dx": (("s", 1, 1), ("r", 1, 3, 2), ("r", 1, 0, 3), ("r", 1, 1, 3),),
+    "dwa": (("s", 1, 2), ("r", 1, 2, 3), ("r", 1, 3, 3), ("r", 0, 0, 1), ("r", 0, 1, 1), ("r", 0, 2, 1), ("r", 0, 3, 1), ("r", 2, 3, 3),),
+    "fb": (("s", 1, 3), ("s", 2, 1),),
+    "tail": (("s", 0, 4), ("r", 0, 0, 2), ("s", 2, 2), ("f", 3, 0), ("r", 0, 1, 2), ("r", 0, 0, 3), ("f", 1, 0), ("f", 3, 1), ("r", 0, 2, 2), ("r", 0, 1, 3), ("f", 1, 1), ("r", 0, 3, 2), ("f", 2, 0), ("r", 0, 2, 3), ("s", 2, 3), ("s", 1, 4), ("r", 0, 3, 3), ("f", 3, 2), ("f", 1, 2), ("f", 2, 1), ("f", 3, 3), ("f", 1, 3), ("f", 2, 2), ("s", 2, 4), ("f", 2, 3), ("f", 0, 0), ("f", 0, 1), ("f", 0, 2), ("f", 0, 3),),
 }
 
 def layer_kernel(
     n_batch, n_head,
-    flags, bounds, x_in, go_in, mc_in, att_in, up_in, down_in, aux_in, norm_in,
-    y_out, dx_out, dqkv_out, dout_out, dmlp_out, small_out,
+    flags, bounds, norm_in, bias_in, map_in, x_in, go_in, mc_in, att_in, up_in, down_in,
+    y_out, dx_out, dqkv_out, dout_out, dmlp_out, small_out, maps_out,
     xs, gos, mcs, wa, wm, aux, nrm,
     xl, qs, ks, vs, mks, mvs, ctx, prob_top, prob_low, hid, x2, acc, dx2,
     u_s, g_s, act_s, du_s, rt_s,
     cwm, um, cen, spr, wsg, isp, nrs, pg, small,
-    got, all_heads, recv, fin, more, links, sems,
+    maps_s, smalls, recv, fin, more, links, sems,
 ):
     gcs, dqs, dks, dvs, gmk, gmv = x2, acc, ks, vs, mks, mvs
     me = lax.axis_index("head")
@@ -402,31 +452,34 @@
         return copy
 
     others = range(1, n_head)
-    net = Exchange(n_batch, n_head, wa, wm, recv, fin, more, links)
+    net = Exchange(n_batch, n_head, wa, wm, recv, fin, more, smalls, links)
     att_copies = [load(att_in, wa.at[:, pl.ds(pl.multiple_of(me * gcols, 16), gcols), :], 5)]
-    aux_own = load(aux_in, aux.at[me], 3)
     copies = [
         load(x_in, xs, 0),
-        load(norm_in, nrm, 1),
         load(mc_in.at[me], mcs, 2),
         load(go_in, gos, 4),
     ]
     mlp_copies = [load(up_in, wm.at[me, 0], 6), load(down_in, wm.at[me, 1], 7)]
+    for row, ref in enumerate(norm_in):
+        nrm[row : row + 1, :] = ref[...].astype(F32).reshape(1, width)
+    aux[me] = jnp.zeros((8, width), F32)
+    for row, ref in enumerate(bias_in[:2]):
+        aux[me, row : row + 1, 0:gcols] = ref[...].astype(F32).reshape(1, gcols)
+    aux[me, 2:3, :] = bias_in[2][...].astype(F32).reshape(1, width)
+    for row, ref in enumerate(map_in):
+        for k in range(ref.shape[0]):
+            aux[me, 3 + row : 4 + row, k * basis : (k + 1) * basis] = ref[k : k + 1, :]
     net.barrier()
     for copy in att_copies:
         copy.wait()
-    for k in others:
-        net.gather_start(ATT, k)
-    aux_own.wait()
+    net.gather_start(ATT)
     for j in range(1, n_head):
         net.aux_copy(aux, j).start()
-    for k in others:
-        net.gather_start(OUT, k)
+    net.gather_start(OUT)
     for copy in mlp_copies:
         copy.wait()
-    for k in others:
-        net.gather_start(UP, k)
-        net.gather_start(DOWN, k)
+    net.gather_start(UP)
+    net.gather_start(DOWN)
 
     def event(op, first, *rest):
         if op == "g":
@@ -436,7 +489,7 @@
         elif op == "f":
             net.final_pass(first, *rest)
         else:
-            net.small_pass(small, got, all_heads, first)
+            net.small_pass(first, *rest)
 
     def take(slot):
         for item in SCHEDULE.get(slot, ()):
@@ -459,7 +512,9 @@
 
         return lax.fori_loop(0, tiles, step, carry)
 
-    small[...] = jnp.zeros_like(small)
+    early, middle, late = (group[0] for group in smalls)
+    for ref in (middle, late):
+        ref[...] = jnp.zeros_like(ref)
     zero_sum = jnp.zeros((8, width), F32)
 
     def mask_rows(span, state):
@@ -485,6 +540,18 @@
     for k in others:
         net.aux_wait(aux, k)
 
+    column = lax.broadcasted_iota(jnp.int32, (1, width), 1)
+    biases = []
+    for row in range(2):
+        bias = jnp.zeros((1, width), F32)
+        for g in range(n_head):
+            moved = aux[g, row : row + 1, :]
+            shift = g * gcols
+            if shift:
+                moved = pltpu.roll(moved, shift, 1)
+            bias = bias + jnp.where(column // gcols == g, moved, 0.0)
+        biases.append(bias)
+
     tile_n = 256
     for kind, out, mem_out, bias_row in ((0, qs, None, 0), (1, ks, mks, None), (2, vs, mvs, 1)):
         for n in range(0, width, tile_n):
@@ -492,15 +559,12 @@
             weight = wa[kind, cols, :]
             value = mm_nt(xl[...], weight)
             if bias_row is not None:
-                bias = aux[0, bias_row : bias_row + 1, cols]
-                for g in range(1, n_head):
-                    bias = bias + aux[g, bias_row : bias_row + 1, cols]
-                value = value + bias
+                value = value + biases[bias_row][:, cols]
             out[:, cols] = value.astype(BF16)
             if mem_out is not None:
                 value = mm_nt(mcs[...], weight)
                 if bias_row is not None:
-                    value = value + bias
+                    value = value + biases[bias_row][:, cols]
                 mem_out[:, cols] = value.astype(BF16)
         take(("proj", kind))
 
@@ -603,7 +667,7 @@
     take("ln2")
 
     def units(k, state):
-        g = lax.rem(me + k, n_head)
+        g = pick(k, net.groups)
         take_at(k, n_head, "needU")
         for n in range(0, width, tile_n):
             cols = slice(n, n + tile_n)
@@ -628,7 +692,7 @@
 
         total = each_tile(activate, zero_sum)
         take_at(k, n_head, "mlp1")
-        small[pl.ds(8 + g, 1), :] = row_sum(total)
+        early[pl.ds(4 + g, 1), :] = row_sum(total)
         for n in range(0, width, tile_n):
             cols = slice(n, n + tile_n)
             acc[:, cols] += mm(act_s[...], wm[g, 1, :, cols])
@@ -680,10 +744,11 @@
 
     sums = each_tile(second_back, (zero_sum,) * 4)
     y_copy = load(du_s, y_out, 0)
-    small[3:4, :] = row_sum(sums[0])
-    small[4:5, :] = row_sum(sums[1])
-    small[2:3, :] = row_sum(sums[2])
-    small[5:6, :] = row_sum(sums[3])
+    early[1:2, :] = row_sum(sums[0])
+    early[2:3, :] = row_sum(sums[1])
+    early[0:1, :] = row_sum(sums[2])
+    early[3:4, :] = row_sum(sums[3])
+    event("s", 0, 0)
     take("sb")
     for n in range(0, width, tile_n):
         cols = slice(n, n + tile_n)
@@ -774,8 +839,8 @@
     weight_grads = sum(mm_nt(piece, mks[...]) for piece in reversed(pieces))
     for h in range(heads):
         g, k = divmod(h, per_group)
-        small[12 + g : 13 + g, k * basis : (k + 1) * basis] = weight_grads[h : h + 1, :]
-        small[16 + g : 17 + g, k * basis : (k + 1) * basis] = weight_grads[16 + h : 17 + h, :]
+        middle[2 + g : 3 + g, k * basis : (k + 1) * basis] = weight_grads[h : h + 1, :]
+        middle[6 + g : 7 + g, k * basis : (k + 1) * basis] = weight_grads[16 + h : 17 + h, :]
     gmk[...] = (
         (mm_tn(parts[1], pieces[0]) + mm_tn(parts[0], pieces[1])) + mm_tn(parts[0], pieces[0])
     ).astype(BF16)
@@ -795,8 +860,9 @@
         )
 
     sums = each_tile(bias_sums, (zero_sum,) * 2)
-    small[6:7, :] = row_sum(sums[0])
-    small[7:8, :] = row_sum(sums[1]) + row_sum(gmv[...].astype(F32))
+    middle[0:1, :] = row_sum(sums[0])
+    middle[1:2, :] = row_sum(sums[1]) + row_sum(gmv[...].astype(F32))
+    event("s", 1, 0)
     take("bias")
 
     for n in range(0, width, tile_n):
@@ -834,9 +900,9 @@
         return (sums[0] + fold8(grad * normed), sums[1] + fold8(grad))
 
     sums = each_tile(first_back, (zero_sum,) * 2)
-    small[0:1, :] = row_sum(sums[0])
-    small[1:2, :] = row_sum(sums[1])
-    event("s", 0)
+    late[0:1, :] = row_sum(sums[0])
+    late[1:2, :] = row_sum(sums[1])
+    event("s", 2, 0)
     outs = [load(du_s, dx_out, 0)]
     take("fb")
     finished = {
@@ -844,12 +910,25 @@
         ("f", OUT, 3): (fin[OUT], dout_out, 2),
         ("f", UP, 3): (fin[UP], dmlp_out.at[pl.ds(0, 1)], 3),
         ("f", DOWN, 3): (fin[DOWN], dmlp_out.at[pl.ds(1, 1)], 4),
-        ("s", 4): (small, small_out, 5),
     }
     for item in SCHEDULE["tail"]:
         event(*item)
         if item in finished:
             outs.append(load(*finished[item]))
+    small[0:2, :] = late[0:2, :]
+    small[2:6, :] = early[0:4, :]
+    small[6:7, :] = early[pl.ds(4 + me, 1), :]
+    for row in range(2):
+        own = middle[row : row + 1, :]
+        for g in range(1, n_head):
+            own = jnp.where(me == g, pltpu.roll(middle[row : row + 1, :], width - g * gcols, 1), own)
+        small[7 + row : 8 + row, :] = own
+    for row in range(2):
+        own = middle[pl.ds(2 + 4 * row + me, 1), :]
+        for k in range(per_group):
+            maps_s[row, k : k + 1, :] = own[:, k * basis : (k + 1) * basis]
+    outs.append(load(maps_s, maps_out, 6))
+    outs.append(load(small, small_out, 5))
     net.all_sent()
     for j in range(1, n_head):
         net.aux_copy(aux, j).wait_send()
@@ -868,21 +947,8 @@
     basis = memory_coefficients.shape[1]
     gcols = query_weight.shape[1]
     heads = centre_weight.shape[0] * n_head
-    me = lax.axis_index("head")
     att = jnp.stack([query_weight.T, key_matrix.T, value_matrix.T, out_weight])
 
-    def spread(vector):
-        return lax.dynamic_update_slice(jnp.zeros((width,), F32), vector.astype(F32), (me * gcols,))
-
-    aux = jnp.stack(
-        [spread(query_bias), spread(value_offset_bias), up_bias.astype(F32),
-         centre_weight.reshape(width), width_weight.reshape(width)]
-    )
-    aux = jnp.pad(aux, ((0, 3), (0, 0)))
-    norm = jnp.stack(
-        [first_gain, first_shift, out_bias, second_gain, second_shift, down_bias]
-    ).astype(F32)
-    norm = jnp.pad(norm, ((0, 2), (0, 0)))
     extra = 0
     while SUB << extra < n_batch:
         extra += 1
@@ -892,12 +958,13 @@
 
     any_spec = pl.BlockSpec(memory_space=pl.ANY)
     smem = pl.BlockSpec(memory_space=pltpu.SMEM)
+    vec = pl.BlockSpec(memory_space=pltpu.VMEM)
     dma = pltpu.SemaphoreType.DMA
     halves = ((3, gcols), (1, gcols), (1, width), (1, width))
     recv = tuple(
         tuple(vm(n_head, t, r // pieces, width // 2) for t, r in halves) for pieces in (1, 2, 4, 4)
     )
-    y, dx, dqkv, dout, dmlp, small = pl.pallas_call(
+    y, dx, dqkv, dout, dmlp, small, maps = pl.pallas_call(
         lambda *refs: layer_kernel(n_batch, n_head, *refs),
         out_shape=(
             jax.ShapeDtypeStruct((rows, width), BF16),
@@ -905,10 +972,11 @@
             jax.ShapeDtypeStruct((3, gcols, width), BF16),
             jax.ShapeDtypeStruct((1, gcols, width), BF16),
             jax.ShapeDtypeStruct((2, width, width), BF16),
-            jax.ShapeDtypeStruct((24, width), F32),
+            jax.ShapeDtypeStruct((16, width), F32),
+            jax.ShapeDtypeStruct((2, heads // n_head, basis), F32),
         ),
-        in_specs=[smem, smem] + [any_spec] * 8,
-        out_specs=[any_spec] * 6,
+        in_specs=[smem, smem, (vec,) * 6, (vec,) * 3, (vec,) * 2] + [any_spec] * 6,
+        out_specs=[any_spec] * 7,
         scratch_shapes=[
             vm(rows, width), vm(rows, width), vm(basis, width),
             vm(4, width, width), vm(n_head, 2, width, width),
@@ -923,32 +991,35 @@
             vm(32, basis, dtype=F32), vm(96, width),
             vm(16, rows, dtype=F32), vm(16, rows, dtype=F32), vm(16, rows, dtype=F32),
             vm(16, rows, dtype=F32), vm(16, rows, dtype=F32), vm(32, rows, dtype=F32),
-            vm(24, width, dtype=F32),
-            vm(3 + extra, 24, width, dtype=F32), vm(n_head, 24, width, dtype=F32),
+            vm(16, width, dtype=F32),
+            vm(2, heads // n_head, basis, dtype=F32),
+            tuple(
+                (vm(r, width, dtype=F32), vm(3 + extra, r, width, dtype=F32),
+                 vm(n_head, r, width, dtype=F32)) for r in (8, 16, 8)
+            ),
             recv,
             tuple(vm(t, r, width) for t, r in halves),
             tuple(vm(extra, t, r // 4, width // 2) for t, r in halves) if extra else (),
-            (dma((4, n_head, 4)), dma((4, n_head, 4)), dma((4, n_head, 4)), dma((4, n_head, 4)),
+            (dma((4, n_head, 4)), dma((4, n_head, 4)), dma((4, n_head)), dma((4, n_head, 4)), dma((4, n_head, 4)),
              dma((4, 3)), dma((4, 3)), dma((4, max(extra, 1))), dma((4, max(extra, 1))),
-             dma((3 + extra + n_head,)),
-             dma((3 + extra + n_head,)), dma((n_head,)), dma((n_head,))),
+             dma((3, 3 + extra + n_head)),
+             dma((3, 3 + extra + n_head)), dma((n_head,)), dma((n_head,))),
             dma((8,)),
         ],
         compiler_params=pltpu.CompilerParams(
             collective_id=0, has_side_effects=True, vmem_limit_bytes=67043328
         ),
-    )(memory_flags, document_start, layer_input, grad_output, memory_coefficients,
-      att, up_weight, down_weight, aux, norm)
-    per_group = heads // n_head
-    mine = lambda row: lax.dynamic_slice(small[row], (me * gcols,), (gcols,))
-    unit = lambda first: lax.dynamic_slice(small, (first + me, 0), (1, width))
+    )(memory_flags, document_start,
+      (first_gain, first_shift, out_bias, second_gain, second_shift, down_bias),
+      (query_bias, value_offset_bias, up_bias), (centre_weight, width_weight),
+      layer_input, grad_output, memory_coefficients, att, up_weight, down_weight)
     return (
         y, dx, small[0], small[1],
-        dqkv[0].T.astype(F32), mine(6), dqkv[1].T.astype(F32), dqkv[2].T.astype(F32), mine(7),
+        dqkv[0].T.astype(F32), small[7, :gcols], dqkv[1].T.astype(F32), dqkv[2].T.astype(F32), small[8, :gcols],
         dout[0].astype(F32),
         small[2], small[3], small[4],
-        dmlp[0].astype(F32), unit(8).reshape(width), dmlp[1].astype(F32), small[5],
-        unit(12).reshape(per_group, basis), unit(16).reshape(per_group, basis),
+        dmlp[0].astype(F32), small[6], dmlp[1].astype(F32), small[5],
+        maps[0], maps[1],
     )
 
 

time: 199 us -> 175 us (0.88)
  Pallas kernels: 174 us -> 159 us
  local copies, waits for them, and re-layouts: 13 us -> 6.53 us
    pallas_call x1, Pallas kernels: 174 us -> 159 us  [per_device(): pl.pallas_call(lambda *refs: layer_kernel(n_batch, n_head, *refs), out_sh...]
    another operation x11 -> x0, local copies, waits for them, and re-layouts: 4.88 us -> none  [the longest x7 4.15 us: per_device(): jnp.stack([first_gain, first_shift, out_bias, second_gain, second_shift,...]
where the time goes in v3:
time: 175 us; the launch traced here: 174 us
  Pallas kernels  159 us (91%)
  other arithmetic  7.75 us (4%)
  local copies, waits for them, and re-layouts  6.53 us (4%)
    pallas_call x1, Pallas kernels, per_device(): pl.pallas_call(lambda *refs: layer_kernel(n_batch, n_head, *refs), out_sh...  159 us

profile of v3, /device:TPU:1, one launch (start us, length us, event | category | flops | bytes accessed | tf_op | source)
XLA Modules:
  0.0 174.3 jit_solution(4005102867610826751)
XLA Ops:
  0.7 2.4 %pad_maximum_fusion.refs_8_ = bf16[4,192,768]{2,1,0:T(8,128)(2,1)} fusion(bf16[1,192,768]{2,1,0:T(8,128)(2,1)} %bitcast.40, bf16[1,192,768]{2,1,0:T(8,128)(2,1)} %bitcast.41, bf16[1,192,768]{2,1,0:T(8,128)(2,1)} %bitcast.42, bf16[1,192,768]{2,1,0:T(8,128)(2,1)} %bitcast.43), kind=kLoop, calls=%fused_computation | loop fusion | flops 1769472 | bytes 2359296 | tf_op jit(solution)/shard_map/stack | solution.py:950
  3.0 159.4 %shard_map.357 = (bf16[512,768]{1,0:T(8,128)(2,1)}, bf16[512,768]{1,0:T(8,128)(2,1)}, bf16[3,192,768]{2,1,0:T(8,128)(2,1)}, bf16[1,192,768]{2,1,0:T(8,128)(2,1)}...) custom-call(s32[4]{0:T(128)} %refs_0_.1, s32[4]{0:T(128)} %refs_1_.1, ...), custom_call_target="tpu_custom_call" | custom-call | tf_op jit(solution)/shard_map/pallas_call | solution.py:967
  162.4 1.3 fusion
  163.7 1.7 slice_reduce_fusion
  165.4 1.3 slice_bitcast_fusion
  166.7 0.0 copy-start
  166.7 2.8 %convert_bitcast_fusion = (f32[768,192]{0,1:T(8,128)}, f32[768,192]{0,1:T(8,128)}, f32[768,192]{0,1:T(8,128)}, f32[192,768]{1,0:T(8,128)}) fusion(bf16[3,192,768]{2,1,0:T(8,128)(2,1)} %get-tuple-element.29, bf16[1,192,768]{2,1,0:T(8,128)(2,1)} %get-tuple-element.30), kind=kLoop, calls=%fused_computation.3 | loop fusion | flops 589824 | bytes 3538944 | tf_op jit(solution)/shard_map/convert_element_type | solution.py:1018
  169.5 0.0 copy-done
  169.5 0.0 copy-start.2
  169.5 2.5 %bitcast_convert_fusion = (f32[768,768]{1,0:T(8,128)}, f32[768,768]{1,0:T(8,128)}) fusion(bf16[2,768,768]{2,1,0:T(8,128)(2,1)S(1)} %copy-done), kind=kLoop, calls=%fused_computation.1 | loop fusion | flops 1179648 | bytes 7077888 | tf_op jit(solution)/shard_map/convert_element_type | solution.py:1021
  172.0 0.0 copy-start.1
  172.0 0.0 copy-done.2
  172.0 0.9 copy.43
  172.9 0.5 copy-done.1
  173.4 0.9 copy.44
Async XLA Ops:
  166.7 2.8 %copy-start = (bf16[2,768,768]{2,1,0:T(8,128)(2,1)S(1)}, bf16[2,768,768]{2,1,0:T(8,128)(2,1)}, u32[]{:S(2)}) copy-start(bf16[2,768,768]{2,1,0:T(8,128)(2,1)} %get-tuple-element.31) | copy-start | bytes 7077892
  169.5 2.6 %copy-start.2 = (bf16[512,768]{1,0:T(8,128)(2,1)S(1)}, bf16[512,768]{1,0:T(8,128)(2,1)}, u32[]{:S(2)}) copy-start(bf16[512,768]{1,0:T(8,128)(2,1)} %get-tuple-element.69) | copy-start | bytes 2359300
  172.0 1.4 copy-start.1

commit v4 on v3

--- a/solution.py
+++ b/solution.py
@@ -53,15 +53,19 @@
     return jnp.sum(value, axis=0, keepdims=True)
 
 
-ATT, OUT, UP, DOWN = range(4)
-KINDS = (ATT, OUT, UP, DOWN)
+ATT, OUT, UP, DOWN, QUERY, KEY, VALUE = range(7)
+SUMMED = (OUT, UP, DOWN, QUERY, KEY, VALUE)
+ALL_GROUPS = (OUT, QUERY, KEY, VALUE)
 DIRECT = (ATT, OUT)
+SPANS = {ATT: (0, 3), OUT: (3, 1), QUERY: (0, 1), KEY: (1, 1), VALUE: (2, 1)}
+EARLY = (DOWN, 1)
 MESH = pl.DeviceIdType.MESH
 SUB = 8
 
 
 def nearest_first(place, count):
-    return sorted(range(count), key=lambda other: (abs(other - place), other))
+    pair = place + 1 - 2 * (place % 2)
+    return sorted(range(count), key=lambda other: (abs(other - place), other != pair))
 
 
 def pick(index, values):
@@ -72,11 +76,11 @@
 
 
 class Exchange:
-    def __init__(self, n_batch, n_head, wa, wm, recv, fin, more, smalls, sems):
-        self.n_head, self.smalls = n_head, smalls
+    def __init__(self, n_batch, n_head, wa, wm, recv, early, fin, more, smalls, sems):
+        self.n_head, self.smalls, self.early = n_head, smalls, early
         self.wa, self.wm = wa, wm
         self.recv, self.fin, self.more = recv, fin, more
-        (self.ag_s, self.ag_r, self.ag_o, self.rs_s, self.rs_r, self.fin_s, self.fin_r, self.ex_s, self.ex_r,
+        (self.ag_s, self.ag_r, self.ag_o, self.early_s, self.early_r, self.rs_s, self.rs_r, self.fin_s, self.fin_r, self.ex_s, self.ex_r,
          self.sm_s, self.sm_r, self.ax_s, self.ax_r) = sems
         b, h = lax.axis_index("batch"), lax.axis_index("head")
         self.b, self.h = b, h
@@ -100,8 +104,12 @@
         self.groups = [
             h if k == 0 else pick(h, [order[k] for order in orders]) for k in range(n_head)
         ]
+        self.places = [
+            pick(h, [orders[orders[place][k]].index(place) for place in range(n_head)])
+            for k in range(n_head)
+        ]
         self.half_width = wm.shape[-1] // 2
-        self.rows = (wa.shape[1] // n_head,) * 2 + (wm.shape[2],) * 2
+        self.rows = [wm.shape[2] if k in (UP, DOWN) else wa.shape[1] // n_head for k in range(7)]
         self.pending = []
 
     def barrier(self):
@@ -123,9 +131,9 @@
 
     def view(self, kind, k, start, count, cols):
         g = self.group(k)
-        if kind >= UP:
+        if kind in (UP, DOWN):
             return self.wm.at[g, pl.ds(kind - UP, 1), pl.ds(pl.multiple_of(start, 16), count), cols]
-        first, many = (0, 3) if kind == ATT else (3, 1)
+        first, many = SPANS[kind]
         offset = pl.multiple_of(g * self.rows[kind] + start, 16)
         return self.wa.at[pl.ds(first, many), pl.ds(offset, count), cols]
 
@@ -167,6 +175,14 @@
             ref, ref, self.ag_o.at[kind, k], self.ag_r.at[kind, g, 0], (self.b, target)
         )
         return copy, (target >= 0) & (target < self.n_head)
+
+    def pass_on(self, kind, k):
+        copy, allowed = self.onward(kind, k)
+
+        @pl.when(allowed)
+        def _():
+            self.gather_step(kind, k, 0, receive=True).wait_recv()
+            copy.start()
 
     def gather_step(self, kind, k, stage, receive=False):
         mine = self.cols(self.core)
@@ -189,10 +205,14 @@
         )
 
     def gather_pass(self, kind, k, stage):
-        self.gather_step(kind, k, stage - 1, receive=True).wait_recv()
+        arrived = self.gather_step(kind, k, stage - 1, receive=True)
         if stage == 1 and kind not in DIRECT:
-            copy, allowed = self.onward(kind, k)
-            pl.when(allowed)(copy.start)
+            for other in range(1, self.n_head):
+                if max(other - 1, 1) == k:
+                    self.pass_on(kind, other)
+            pl.when(jnp.logical_not(self.onward(kind, k)[1]))(arrived.wait_recv)
+        else:
+            arrived.wait_recv()
         if stage < 4:
             self.gather_step(kind, k, stage).start()
 
@@ -222,9 +242,9 @@
             src, peer = self.part(kind, k, 4, self.quarter, mine), (self.b, self.group(k))
         at = k
         if stage == 3 and not receive:
-            at = lax.rem(self.h - self.group(k) + self.n_head, self.n_head)
+            at = self.places[k]
         return self.copy(
-            src, self.recv[stage][kind].at[at], self.rs_s.at[kind, k, stage],
+            src, self.recv[stage][kind - 1].at[at], self.rs_s.at[kind, k, stage],
             self.rs_r.at[kind, at, stage], peer,
         )
 
@@ -232,7 +252,7 @@
         mine = self.cols(self.core)
         own = self.view(kind, k, start, count, mine)
         target = own if out is None else out
-        sources = [buf.at[k, :, pl.ds(pl.multiple_of(start - base, 16), count), :] for buf, base in received]
+        sources = [buf.at[:, pl.ds(pl.multiple_of(start - base, 16), count), :] for buf, base in received]
         kinds = own.shape[0]
         tile = min(count, 192)
 
@@ -250,30 +270,47 @@
 
             lax.fori_loop(0, count // tile, step, 0)
 
+    def early_copy(self):
+        kind, k = EARLY
+        src = self.part(kind, k, 1, 0, self.cols(self.core))
+        return self.copy(
+            src, self.early.at[0], self.early_s, self.early_r, (self.b, self.group(k))
+        )
+
     def reduce_pass(self, kind, k, stage):
         rows = self.rows[kind]
         half, quarter = rows // 2, rows // 4
-        first, second, third = (self.recv[s][kind] for s in range(3))
+        first, second, third = (self.recv[s][kind - 1].at[k] for s in range(3))
         if stage > 0:
             self.reduce_step(kind, k, stage - 1).wait_recv()
+        if (kind, k) == EARLY and stage == 1:
+            self.add_rows(kind, k, 0, rows, [(first, 0)])
+            self.early_copy().start()
+            return
         kept = self.high * half
+        parts = [(first, 0)]
+        if kind == EARLY[0] and k == 0:
+            parts.append((self.early.at[0], 0))
+            if stage == 1:
+                self.early_copy().wait_recv()
         if stage == 1:
-            self.add_rows(kind, k, (1 - self.high) * half, half, [(first, 0)])
+            self.add_rows(kind, k, (1 - self.high) * half, half, parts)
         elif stage == 2:
             self.add_rows(
-                kind, k, self.other_quarter * quarter, quarter, [(first, 0), (second, kept)]
+                kind, k, self.other_quarter * quarter, quarter, parts + [(second, kept)]
             )
         elif stage == 3:
             own = self.quarter * quarter
-            self.add_rows(
-                kind, k, own, quarter, [(first, 0), (second, kept), (third, own)]
-            )
+            self.add_rows(kind, k, own, quarter, parts + [(second, kept), (third, own)])
         if stage < 3 or k > 0:
             self.reduce_step(kind, k, stage).start()
 
+    def late(self, kind):
+        return [k for k in range(1, self.n_head) if (kind, k) != EARLY]
+
     def fin_part(self, kind, pieces, index, cols):
         count = self.rows[kind] // pieces
-        return self.fin[kind].at[:, pl.ds(pl.multiple_of(index * count, 16), count), cols]
+        return self.fin[kind - 1].at[:, pl.ds(pl.multiple_of(index * count, 16), count), cols]
 
     def final_step(self, kind, stage, receive=False):
         mine = self.cols(self.core)
@@ -290,10 +327,10 @@
 
     def final_pass(self, kind, stage):
         if stage == 0:
-            for k in range(1, self.n_head):
+            for k in self.late(kind):
                 self.reduce_step(kind, k, 3, receive=True).wait_recv()
             quarter = self.rows[kind] // 4
-            last = self.recv[3][kind]
+            last = self.recv[3][kind - 1]
             mine = self.cols(self.core)
             own = self.view(kind, 0, self.quarter * quarter, quarter, mine)
             target = self.fin_part(kind, 4, self.quarter, mine)
@@ -302,7 +339,7 @@
                 def step(i, state):
                     span = pl.ds(pl.multiple_of(i * tile, 16), tile)
                     total = own[t, span, :].astype(F32)
-                    for k in range(1, self.n_head):
+                    for k in self.late(kind):
                         total = total + last[k, t, span, :].astype(F32)
                     target[t, span, :] = total.astype(BF16)
                     return state
@@ -310,13 +347,13 @@
                 lax.fori_loop(0, quarter // tile, step, 0)
             for e, peer in enumerate(self.extra):
                 copy = self.copy(
-                    target, self.more[kind].at[e], self.ex_s.at[kind, e], self.ex_r.at[kind, e],
+                    target, self.more[kind - 1].at[e], self.ex_s.at[kind, e], self.ex_r.at[kind, e],
                     (peer, self.h),
                 )
                 copy.start()
                 copy.wait()
                 for t in range(own.shape[0]):
-                    total = target[t].astype(F32) + self.more[kind][e, t].astype(F32)
+                    total = target[t].astype(F32) + self.more[kind - 1][e, t].astype(F32)
                     target[t] = total.astype(BF16)
         else:
             self.final_step(kind, stage - 1, receive=True).wait_recv()
@@ -324,11 +361,12 @@
             self.final_step(kind, stage).start()
 
     def all_sent(self):
-        for kind in KINDS:
+        self.early_copy().wait_send()
+        for kind in SUMMED:
             for k in range(self.n_head):
-                for stage in range(4):
-                    if stage < 3 or k > 0:
-                        self.reduce_step(kind, k, stage).wait_send()
+                stages = range(1) if (kind, k) == EARLY else range(4 if k > 0 else 3)
+                for stage in stages:
+                    self.reduce_step(kind, k, stage).wait_send()
             for stage in range(3):
                 self.final_step(kind, stage).wait_send()
 
@@ -383,42 +421,44 @@
 
 
 SCHEDULE = {
-    "needA": (("g", 0, 1, 1), ("g", 0, 1, 2), ("g", 0, 2, 1), ("g", 1, 1, 1), ("g", 0, 3, 1), ("g", 1, 2, 1), ("g", 0, 1, 3), ("g", 0, 2, 2), ("g", 1, 1, 2), ("g", 0, 1, 4), ("g", 1, 3, 1), ("g", 0, 3, 2), ("g", 1, 2, 2), ("g", 2, 1, 1), ("g", 0, 2, 3), ("g", 1, 3, 2), ("g", 1, 1, 3), ("g", 0, 2, 4), ("g", 3, 1, 1), ("g", 2, 2, 1), ("g", 0, 3, 3), ("g", 2, 1, 2), ("g", 1, 2, 3), ("g", 0, 3, 4),),
+    "needA": (("g", 0, 1, 1), ("g", 0, 1, 2), ("g", 0, 2, 1), ("g", 1, 2, 1), ("g", 0, 3, 1), ("g", 1, 1, 1), ("g", 0, 1, 3), ("g", 0, 2, 2), ("g", 1, 2, 2), ("g", 0, 1, 4), ("g", 1, 3, 1), ("g", 0, 3, 2), ("g", 1, 1, 2), ("g", 0, 2, 3), ("g", 1, 3, 2), ("g", 2, 1, 1), ("g", 1, 2, 3), ("g", 0, 2, 4), ("g", 3, 1, 1), ("g", 2, 2, 1), ("g", 0, 3, 3), ("g", 2, 1, 2), ("g", 1, 1, 3), ("g", 0, 3, 4),),
     ("proj", 0): (("g", 3, 2, 1),),
-    ("proj", 1): (("g", 1, 3, 3), ("g", 3, 1, 2),),
-    ("fwd", 0): (("g", 2, 2, 2), ("g", 2, 3, 1),),
+    ("proj", 1): (("g", 1, 3, 3),),
+    ("proj", 2): (("g", 3, 1, 2),),
+    ("fwd", 1): (("g", 2, 2, 2), ("g", 2, 3, 1),),
     ("fwd", 3): (("g", 2, 1, 3), ("g", 3, 2, 2), ("g", 3, 3, 1),),
-    ("fwd", 5): (("g", 2, 3, 2),),
-    "needO": (("g", 1, 1, 4), ("g", 1, 2, 4), ("g", 1, 3, 4),),
-    ("mlp0", 0): (("g", 3, 1, 3), ("g", 3, 3, 2),),
+    "needO": (("g", 1, 2, 4), ("g", 1, 1, 4), ("g", 1, 3, 4),),
+    "out": (("g", 2, 3, 2),),
+    ("mlp0", 0): (("g", 3, 1, 3),),
+    ("mlp1", 0): (("g", 3, 3, 2),),
     ("mlp2", 0): (("g", 2, 2, 3),),
     ("needU", 1): (("g", 2, 1, 4),),
-    ("mlp0", 1): (("g", 3, 2, 3), ("r", 3, 0, 1),),
+    ("mlp0", 1): (("g", 3, 2, 3),),
     ("needD", 1): (("g", 3, 1, 4),),
-    ("mlp1", 1): (("g", 2, 3, 3), ("r", 2, 0, 1),),
-    ("mlpU", 1): (("g", 3, 3, 3),),
+    ("mlp1", 1): (("r", 2, 0, 1),),
+    ("mlp2", 1): (("g", 2, 3, 3),),
     ("needU", 2): (("g", 2, 2, 4),),
-    ("mlp0", 2): (("r", 3, 1, 1), ("r", 2, 1, 1),),
+    ("mlp0", 2): (("g", 3, 3, 3), ("r", 3, 1, 1),),
     ("needD", 2): (("g", 3, 2, 4),),
-    ("mlp1", 2): (("r", 3, 0, 2),),
-    ("mlp2", 2): (("r", 2, 0, 2),),
+    ("mlp1", 2): (("r", 2, 0, 2), ("r", 2, 1, 1),),
     ("needU", 3): (("g", 2, 3, 4),),
-    ("mlp0", 3): (("r", 3, 2, 1), ("r", 2, 2, 1), ("r", 3, 0, 3),),
+    ("mlp0", 3): (("r", 3, 2, 1), ("r", 2, 2, 1), ("r", 2, 0, 3),),
     ("needD", 3): (("g", 3, 3, 4),),
-    ("mlp2", 3): (("r", 3, 1, 2), ("r", 2, 0, 3),),
-    ("mlpU", 3): (("r", 2, 1, 2),),
-    "sb": (("r", 3, 3, 1), ("r", 2, 3, 1),),
-    "gctx": (("r", 3, 1, 3), ("s", 0, 1),),
-    ("bwd0", 0): (("r", 3, 2, 2), ("r", 2, 1, 3), ("s", 0, 2), ("r", 1, 0, 1), ("r", 1, 1, 1), ("r", 1, 2, 1), ("r", 1, 3, 1),),
-    ("bwd0", 2): (("r", 3, 2, 3), ("r", 2, 2, 2),),
-    ("bwd1", 3): (("r", 3, 3, 2),),
-    ("bwd1", 4): (("r", 2, 2, 3),),
-    "mem": (("s", 0, 3), ("r", 1, 0, 2), ("r", 3, 3, 3), ("r", 1, 1, 2), ("r", 2, 3, 2),),
-    "bias": (("r", 1, 2, 2),),
-    "dx": (("s", 1, 1), ("r", 1, 3, 2), ("r", 1, 0, 3), ("r", 1, 1, 3),),
-    "dwa": (("s", 1, 2), ("r", 1, 2, 3), ("r", 1, 3, 3), ("r", 0, 0, 1), ("r", 0, 1, 1), ("r", 0, 2, 1), ("r", 0, 3, 1), ("r", 2, 3, 3),),
-    "fb": (("s", 1, 3), ("s", 2, 1),),
-    "tail": (("s", 0, 4), ("r", 0, 0, 2), ("s", 2, 2), ("f", 3, 0), ("r", 0, 1, 2), ("r", 0, 0, 3), ("f", 1, 0), ("f", 3, 1), ("r", 0, 2, 2), ("r", 0, 1, 3), ("f", 1, 1), ("r", 0, 3, 2), ("f", 2, 0), ("r", 0, 2, 3), ("s", 2, 3), ("s", 1, 4), ("r", 0, 3, 3), ("f", 3, 2), ("f", 1, 2), ("f", 2, 1), ("f", 3, 3), ("f", 1, 3), ("f", 2, 2), ("s", 2, 4), ("f", 2, 3), ("f", 0, 0), ("f", 0, 1), ("f", 0, 2), ("f", 0, 3),),
+    ("mlp1", 3): (("r", 2, 1, 2),),
+    ("mlpD", 3): (("r", 3, 2, 2),),
+    "sb": (("r", 2, 3, 1), ("r", 2, 1, 3), ("r", 3, 0, 1), ("r", 3, 3, 1),),
+    "dwo": (("r", 2, 2, 2), ("s", 0, 1), ("r", 3, 2, 3),),
+    ("bwd0", 0): (("r", 1, 0, 1),),
+    ("bwd0", 1): (("r", 2, 3, 2),),
+    ("bwd1", 1): (("r", 2, 2, 3), ("s", 0, 2),),
+    ("bwd1", 3): (("r", 3, 0, 2), ("r", 2, 3, 3),),
+    ("bwd0", 5): (("r", 3, 3, 2),),
+    "dwv": (("r", 3, 0, 3), ("r", 6, 0, 1),),
+    "mem": (("s", 0, 3), ("r", 1, 0, 2), ("r", 3, 3, 3),),
+    "dwk": (("s", 1, 1), ("f", 2, 0), ("r", 5, 0, 1),),
+    "dwq": (("s", 1, 2), ("r", 6, 0, 2), ("r", 4, 0, 1), ("r", 1, 0, 3),),
+    "fb": (("s", 2, 1),),
+    "tail": (("s", 0, 4), ("f", 2, 1), ("r", 5, 0, 2), ("r", 6, 0, 3), ("f", 3, 0), ("s", 2, 2), ("s", 1, 3), ("f", 1, 0), ("r", 5, 0, 3), ("r", 4, 0, 2), ("f", 6, 0), ("f", 3, 1), ("f", 1, 1), ("r", 4, 0, 3), ("s", 1, 4), ("f", 2, 2), ("f", 6, 1), ("s", 2, 3), ("f", 2, 3), ("f", 5, 0), ("f", 3, 2), ("f", 1, 2), ("f", 5, 1), ("f", 3, 3), ("f", 6, 2), ("f", 1, 3), ("f", 4, 0), ("f", 6, 3), ("f", 5, 2), ("s", 2, 4), ("f", 4, 1), ("f", 5, 3), ("f", 4, 2), ("f", 4, 3),),
 }
 
 def layer_kernel(
@@ -429,7 +469,7 @@
     xl, qs, ks, vs, mks, mvs, ctx, prob_top, prob_low, hid, x2, acc, dx2,
     u_s, g_s, act_s, du_s, rt_s,
     cwm, um, cen, spr, wsg, isp, nrs, pg, small,
-    maps_s, smalls, recv, fin, more, links, sems,
+    maps_s, smalls, recv, ahead, fin, more, links, sems,
 ):
     gcs, dqs, dks, dvs, gmk, gmv = x2, acc, ks, vs, mks, mvs
     me = lax.axis_index("head")
@@ -452,7 +492,7 @@
         return copy
 
     others = range(1, n_head)
-    net = Exchange(n_batch, n_head, wa, wm, recv, fin, more, smalls, links)
+    net = Exchange(n_batch, n_head, wa, wm, recv, ahead, fin, more, smalls, links)
     att_copies = [load(att_in, wa.at[:, pl.ds(pl.multiple_of(me * gcols, 16), gcols), :], 5)]
     copies = [
         load(x_in, xs, 0),
@@ -485,7 +525,9 @@
         if op == "g":
             net.gather_pass(first, *rest)
         elif op == "r":
-            net.reduce_pass(first, *rest)
+            group, stage = rest
+            for k in range(n_head) if first in ALL_GROUPS else (group,):
+                net.reduce_pass(first, k, stage)
         elif op == "f":
             net.final_pass(first, *rest)
         else:
@@ -759,8 +801,7 @@
     for n in range(0, width, tile_n):
         cols = slice(n, n + tile_n)
         wa[3, :, cols] = mm_tn(ctx[...], act_s[:, cols]).astype(BF16)
-    for k in range(n_head):
-        net.reduce_pass(OUT, k, 0)
+    event("r", OUT, 0, 0)
     take("dwo")
 
     def backward_pair(p, state):
@@ -832,6 +873,27 @@
     lax.fori_loop(0, pairs, backward_pair, 0)
     y_copy.wait()
 
+    def input_share(kind, grads, first):
+        for n in range(0, width, tile_n):
+            cols = slice(n, n + tile_n)
+            value = mm(grads[...], wa[kind, :, cols])
+            dx2[:, cols] = value if first else dx2[:, cols] + value
+
+    def weight_share(kind, grads, memory):
+        for n in range(0, width, tile_n):
+            cols = slice(n, n + tile_n)
+            value = mm_tn(grads[...], xl[:, cols])
+            if memory is not None:
+                value = value + mm_tn(memory[...], mcs[:, cols])
+            wa[kind, :, cols] = value.astype(BF16)
+
+    for k in range(n_head):
+        net.gather_sent(ATT, k)
+    input_share(2, dvs, True)
+    weight_share(2, dvs, gmv)
+    event("r", VALUE, 0, 0)
+    take("dwv")
+
     slopes = three_parts(pg[...])
     moments = sum(mm(part, qs[...]) for part in reversed(slopes))
     moments = jnp.where(own_lanes, moments * scale, 0.0)
@@ -865,29 +927,14 @@
     event("s", 1, 0)
     take("bias")
 
-    for n in range(0, width, tile_n):
-        cols = slice(n, n + tile_n)
-        dx2[:, cols] = (
-            mm(act_s[...], wa[0, :, cols])
-            + mm(dks[...], wa[1, :, cols])
-            + mm(dvs[...], wa[2, :, cols])
-        )
-    take("dx")
-    for k in range(n_head):
-        net.gather_sent(ATT, k)
-    for n in range(0, width, tile_n):
-        cols = slice(n, n + tile_n)
-        wa[0, :, cols] = mm_tn(act_s[...], xl[:, cols]).astype(BF16)
-        wa[1, :, cols] = (
-            mm_tn(dks[...], xl[:, cols]) + mm_tn(gmk[...], mcs[:, cols])
-        ).astype(BF16)
-        wa[2, :, cols] = (
-            mm_tn(dvs[...], xl[:, cols]) + mm_tn(gmv[...], mcs[:, cols])
-        ).astype(BF16)
-
-    for k in range(n_head):
-        net.reduce_pass(ATT, k, 0)
-    take("dwa")
+    input_share(1, dks, False)
+    weight_share(1, dks, gmk)
+    event("r", KEY, 0, 0)
+    take("dwk")
+    input_share(0, act_s, False)
+    weight_share(0, act_s, None)
+    event("r", QUERY, 0, 0)
+    take("dwq")
 
     def first_back(span, sums):
         normed, factor = norm_rows(xs[span, :].astype(F32))
@@ -906,15 +953,18 @@
     outs = [load(du_s, dx_out, 0)]
     take("fb")
     finished = {
-        ("f", ATT, 3): (fin[ATT], dqkv_out, 1),
-        ("f", OUT, 3): (fin[OUT], dout_out, 2),
-        ("f", UP, 3): (fin[UP], dmlp_out.at[pl.ds(0, 1)], 3),
-        ("f", DOWN, 3): (fin[DOWN], dmlp_out.at[pl.ds(1, 1)], 4),
+        ("f", QUERY, 3): (QUERY, dqkv_out.at[pl.ds(0, 1)], 1),
+        ("f", KEY, 3): (KEY, dqkv_out.at[pl.ds(1, 1)], 2),
+        ("f", VALUE, 3): (VALUE, dqkv_out.at[pl.ds(2, 1)], 3),
+        ("f", OUT, 3): (OUT, dout_out, 4),
+        ("f", UP, 3): (UP, dmlp_out.at[pl.ds(0, 1)], 7),
+        ("f", DOWN, 3): (DOWN, dmlp_out.at[pl.ds(1, 1)], 8),
     }
     for item in SCHEDULE["tail"]:
         event(*item)
         if item in finished:
-            outs.append(load(*finished[item]))
+            kind, target, at = finished[item]
+            outs.append(load(fin[kind - 1], target, at))
     small[0:2, :] = late[0:2, :]
     small[2:6, :] = early[0:4, :]
     small[6:7, :] = early[pl.ds(4 + me, 1), :]
@@ -960,7 +1010,7 @@
     smem = pl.BlockSpec(memory_space=pltpu.SMEM)
     vec = pl.BlockSpec(memory_space=pltpu.VMEM)
     dma = pltpu.SemaphoreType.DMA
-    halves = ((3, gcols), (1, gcols), (1, width), (1, width))
+    halves = ((1, gcols), (1, width), (1, width)) + ((1, gcols),) * 3
     recv = tuple(
         tuple(vm(n_head, t, r // pieces, width // 2) for t, r in halves) for pieces in (1, 2, 4, 4)
     )
@@ -997,14 +1047,14 @@
                 (vm(r, width, dtype=F32), vm(3 + extra, r, width, dtype=F32),
                  vm(n_head, r, width, dtype=F32)) for r in (8, 16, 8)
             ),
-            recv,
+            recv, vm(1, 1, width, width // 2),
             tuple(vm(t, r, width) for t, r in halves),
             tuple(vm(extra, t, r // 4, width // 2) for t, r in halves) if extra else (),
-            (dma((4, n_head, 4)), dma((4, n_head, 4)), dma((4, n_head)), dma((4, n_head, 4)), dma((4, n_head, 4)),
-             dma((4, 3)), dma((4, 3)), dma((4, max(extra, 1))), dma((4, max(extra, 1))),
+            (dma((4, n_head, 4)), dma((4, n_head, 4)), dma((4, n_head)), dma, dma, dma((7, n_head, 4)), dma((7, n_head, 4)),
+             dma((7, 3)), dma((7, 3)), dma((7, max(extra, 1))), dma((7, max(extra, 1))),
              dma((3, 3 + extra + n_head)),
              dma((3, 3 + extra + n_head)), dma((n_head,)), dma((n_head,))),
-            dma((8,)),
+            dma((10,)),
         ],
         compiler_params=pltpu.CompilerParams(
             collective_id=0, has_side_effects=True, vmem_limit_bytes=67043328

time: 175 us -> 165 us (0.943)
  Pallas kernels: 159 us -> 150 us
    pallas_call x1, Pallas kernels: 159 us -> 150 us  [per_device(): pl.pallas_call(lambda *refs: layer_kernel(n_batch, n_head, *refs), out_sh...]
where the time goes in v4:
time: 165 us
  Pallas kernels  150 us (91%)
  other arithmetic  7.75 us (5%)
  local copies, waits for them, and re-layouts  6.53 us (4%)
    pallas_call x1, Pallas kernels, per_device(): pl.pallas_call(lambda *refs: layer_kernel(n_batch, n_head, *refs), out_sh...  150 us

profile of v4, /device:TPU:1, one launch (start us, length us, event | category | flops | bytes accessed | tf_op | source)
XLA Modules:
  0.0 164.7 jit_solution(2297759377017439843)
XLA Ops:
  0.7 2.4 %pad_maximum_fusion.refs_8_ = bf16[4,192,768]{2,1,0:T(8,128)(2,1)} fusion(bf16[1,192,768]{2,1,0:T(8,128)(2,1)} %bitcast.40, bf16[1,192,768]{2,1,0:T(8,128)(2,1)} %bitcast.41, bf16[1,192,768]{2,1,0:T(8,128)(2,1)} %bitcast.42, bf16[1,192,768]{2,1,0:T(8,128)(2,1)} %bitcast.43), kind=kLoop, calls=%fused_computation | loop fusion | flops 1769472 | bytes 2359296 | tf_op jit(solution)/shard_map/stack | solution.py:1000
  3.0 149.7 %shard_map.357 = (bf16[512,768]{1,0:T(8,128)(2,1)}, bf16[512,768]{1,0:T(8,128)(2,1)}, bf16[3,192,768]{2,1,0:T(8,128)(2,1)}, bf16[1,192,768]{2,1,0:T(8,128)(2,1)}...) custom-call(s32[4]{0:T(128)} %refs_0_.1, s32[4]{0:T(128)} %refs_1_.1, ...), custom_call_target="tpu_custom_call" | custom-call | tf_op jit(solution)/shard_map/pallas_call | solution.py:1017
  152.8 1.3 fusion
  154.1 1.7 %slice_reduce_fusion = (f32[768]{0:T(1024)}, f32[768]{0:T(1024)}, f32[768]{0:T(1024)}, f32[768]{0:T(1024)}, f32[768]{0:T(1024)}, /*index=5*/f32[768]{0:T(1024)}, f32[768]{0:T(1024)}) fusion(f32[16,768]{1,0:T(8,128)} %get-tuple-element.28), kind=kLoop, calls=%fused_computation.9 | loop fusion | bytes 43008 | tf_op jit(solution)/shard_map/slice | solution.py:1071
  155.7 1.3 slice_bitcast_fusion
  157.0 0.0 copy-start
  157.0 2.8 %convert_bitcast_fusion = (f32[768,192]{0,1:T(8,128)}, f32[768,192]{0,1:T(8,128)}, f32[768,192]{0,1:T(8,128)}, f32[192,768]{1,0:T(8,128)}) fusion(bf16[3,192,768]{2,1,0:T(8,128)(2,1)} %get-tuple-element.29, bf16[1,192,768]{2,1,0:T(8,128)(2,1)} %get-tuple-element.30), kind=kLoop, calls=%fused_computation.3 | loop fusion | flops 589824 | bytes 3538944 | tf_op jit(solution)/shard_map/convert_element_type | solution.py:1068
  159.8 0.0 copy-done
  159.8 0.0 copy-start.2
  159.8 2.5 %bitcast_convert_fusion = (f32[768,768]{1,0:T(8,128)}, f32[768,768]{1,0:T(8,128)}) fusion(bf16[2,768,768]{2,1,0:T(8,128)(2,1)S(1)} %copy-done), kind=kLoop, calls=%fused_computation.1 | loop fusion | flops 1179648 | bytes 7077888 | tf_op jit(solution)/shard_map/convert_element_type | solution.py:1071
  162.4 0.0 copy-start.1
  162.4 0.0 copy-done.2
  162.4 0.9 copy.43
  163.3 0.5 copy-done.1
  163.8 0.9 copy.44
Async XLA Ops:
  157.0 2.8 %copy-start = (bf16[2,768,768]{2,1,0:T(8,128)(2,1)S(1)}, bf16[2,768,768]{2,1,0:T(8,128)(2,1)}, u32[]{:S(2)}) copy-start(bf16[2,768,768]{2,1,0:T(8,128)(2,1)} %get-tuple-element.31) | copy-start | bytes 7077892
  159.8 2.6 %copy-start.2 = (bf16[512,768]{1,0:T(8,128)(2,1)S(1)}, bf16[512,768]{1,0:T(8,128)(2,1)}, u32[]{:S(2)}) copy-start(bf16[512,768]{1,0:T(8,128)(2,1)} %get-tuple-element.69) | copy-start | bytes 2359300
  162.4 1.4 copy-start.1

commit v5 on v4

--- a/solution.py
+++ b/solution.py
@@ -12,7 +12,7 @@
 EPS = 1e-05
 ROOT = math.sqrt(2.0 / math.pi)
 CUBE = 0.044715
-ROW_TILE = 128
+ROW_TILE = 256
 
 
 def mm(left, right):
@@ -421,44 +421,43 @@
 
 
 SCHEDULE = {
-    "needA": (("g", 0, 1, 1), ("g", 0, 1, 2), ("g", 0, 2, 1), ("g", 1, 2, 1), ("g", 0, 3, 1), ("g", 1, 1, 1), ("g", 0, 1, 3), ("g", 0, 2, 2), ("g", 1, 2, 2), ("g", 0, 1, 4), ("g", 1, 3, 1), ("g", 0, 3, 2), ("g", 1, 1, 2), ("g", 0, 2, 3), ("g", 1, 3, 2), ("g", 2, 1, 1), ("g", 1, 2, 3), ("g", 0, 2, 4), ("g", 3, 1, 1), ("g", 2, 2, 1), ("g", 0, 3, 3), ("g", 2, 1, 2), ("g", 1, 1, 3), ("g", 0, 3, 4),),
+    "needA": (("g", 0, 1, 1), ("g", 0, 1, 2), ("g", 0, 2, 1), ("g", 1, 2, 1), ("g", 0, 3, 1), ("g", 1, 1, 1), ("g", 0, 1, 3), ("g", 0, 2, 2), ("g", 1, 2, 2), ("g", 0, 1, 4), ("g", 0, 3, 2), ("g", 1, 3, 1), ("g", 1, 1, 2), ("g", 2, 1, 1), ("g", 0, 2, 3), ("g", 1, 3, 2), ("g", 1, 2, 3), ("g", 0, 2, 4), ("g", 3, 1, 1), ("g", 2, 2, 1), ("g", 0, 3, 3), ("g", 2, 1, 2), ("g", 1, 1, 3), ("g", 0, 3, 4),),
     ("proj", 0): (("g", 3, 2, 1),),
-    ("proj", 1): (("g", 1, 3, 3),),
-    ("proj", 2): (("g", 3, 1, 2),),
-    ("fwd", 1): (("g", 2, 2, 2), ("g", 2, 3, 1),),
-    ("fwd", 3): (("g", 2, 1, 3), ("g", 3, 2, 2), ("g", 3, 3, 1),),
+    ("proj", 1): (("g", 1, 3, 3), ("g", 3, 1, 2),),
+    ("fwd", 0): (("g", 2, 3, 1),),
+    ("fwd", 1): (("g", 2, 2, 2),),
+    ("fwd", 2): (("g", 2, 1, 3),),
+    ("fwd", 3): (("g", 3, 2, 2), ("g", 3, 3, 1),),
+    ("fwd", 5): (("g", 2, 3, 2),),
     "needO": (("g", 1, 2, 4), ("g", 1, 1, 4), ("g", 1, 3, 4),),
-    "out": (("g", 2, 3, 2),),
-    ("mlp0", 0): (("g", 3, 1, 3),),
-    ("mlp1", 0): (("g", 3, 3, 2),),
+    ("mlp0", 0): (("g", 3, 1, 3), ("g", 3, 3, 2),),
     ("mlp2", 0): (("g", 2, 2, 3),),
     ("needU", 1): (("g", 2, 1, 4),),
     ("mlp0", 1): (("g", 3, 2, 3),),
     ("needD", 1): (("g", 3, 1, 4),),
-    ("mlp1", 1): (("r", 2, 0, 1),),
-    ("mlp2", 1): (("g", 2, 3, 3),),
+    ("mlp1", 1): (("r", 2, 0, 1), ("g", 2, 3, 3),),
+    ("mlpU", 1): (("g", 3, 3, 3),),
     ("needU", 2): (("g", 2, 2, 4),),
-    ("mlp0", 2): (("g", 3, 3, 3), ("r", 3, 1, 1),),
+    ("mlp0", 2): (("r", 3, 1, 1), ("r", 2, 1, 1),),
     ("needD", 2): (("g", 3, 2, 4),),
-    ("mlp1", 2): (("r", 2, 0, 2), ("r", 2, 1, 1),),
+    ("mlp1", 2): (("r", 2, 0, 2),),
     ("needU", 3): (("g", 2, 3, 4),),
-    ("mlp0", 3): (("r", 3, 2, 1), ("r", 2, 2, 1), ("r", 2, 0, 3),),
+    ("mlp0", 3): (("r", 2, 1, 2), ("r", 2, 0, 3), ("r", 2, 2, 1), ("r", 3, 2, 1),),
     ("needD", 3): (("g", 3, 3, 4),),
-    ("mlp1", 3): (("r", 2, 1, 2),),
-    ("mlpD", 3): (("r", 3, 2, 2),),
-    "sb": (("r", 2, 3, 1), ("r", 2, 1, 3), ("r", 3, 0, 1), ("r", 3, 3, 1),),
-    "dwo": (("r", 2, 2, 2), ("s", 0, 1), ("r", 3, 2, 3),),
-    ("bwd0", 0): (("r", 1, 0, 1),),
-    ("bwd0", 1): (("r", 2, 3, 2),),
-    ("bwd1", 1): (("r", 2, 2, 3), ("s", 0, 2),),
-    ("bwd1", 3): (("r", 3, 0, 2), ("r", 2, 3, 3),),
-    ("bwd0", 5): (("r", 3, 3, 2),),
-    "dwv": (("r", 3, 0, 3), ("r", 6, 0, 1),),
-    "mem": (("s", 0, 3), ("r", 1, 0, 2), ("r", 3, 3, 3),),
-    "dwk": (("s", 1, 1), ("f", 2, 0), ("r", 5, 0, 1),),
-    "dwq": (("s", 1, 2), ("r", 6, 0, 2), ("r", 4, 0, 1), ("r", 1, 0, 3),),
-    "fb": (("s", 2, 1),),
-    "tail": (("s", 0, 4), ("f", 2, 1), ("r", 5, 0, 2), ("r", 6, 0, 3), ("f", 3, 0), ("s", 2, 2), ("s", 1, 3), ("f", 1, 0), ("r", 5, 0, 3), ("r", 4, 0, 2), ("f", 6, 0), ("f", 3, 1), ("f", 1, 1), ("r", 4, 0, 3), ("s", 1, 4), ("f", 2, 2), ("f", 6, 1), ("s", 2, 3), ("f", 2, 3), ("f", 5, 0), ("f", 3, 2), ("f", 1, 2), ("f", 5, 1), ("f", 3, 3), ("f", 6, 2), ("f", 1, 3), ("f", 4, 0), ("f", 6, 3), ("f", 5, 2), ("s", 2, 4), ("f", 4, 1), ("f", 5, 3), ("f", 4, 2), ("f", 4, 3),),
+    ("mlpD", 3): (("r", 2, 1, 3),),
+    "sb": (("r", 2, 2, 2), ("r", 2, 3, 1), ("r", 3, 0, 1), ("r", 3, 3, 1),),
+    "gctx": (("r", 3, 2, 2),),
+    "dwo": (("s", 0, 1),),
+    ("bwd1", 0): (("r", 2, 2, 3), ("r", 1, 0, 1),),
+    ("bwd0", 2): (("r", 2, 3, 2), ("s", 0, 2), ("r", 3, 2, 3),),
+    ("bwd1", 3): (("r", 3, 0, 2),),
+    ("bwd1", 4): (("r", 2, 3, 3),),
+    "dwv": (("r", 3, 3, 2), ("r", 3, 0, 3), ("r", 6, 0, 1),),
+    "mem": (("s", 0, 3), ("r", 1, 0, 2),),
+    "dwk": (("s", 1, 1), ("r", 3, 3, 3), ("r", 5, 0, 1),),
+    "dwq": (("r", 1, 0, 3), ("f", 2, 0), ("r", 4, 0, 1), ("r", 6, 0, 2),),
+    "fb": (("s", 1, 2), ("s", 2, 1),),
+    "tail": (("s", 0, 4), ("r", 5, 0, 2), ("f", 2, 1), ("r", 6, 0, 3), ("s", 2, 2), ("f", 3, 0), ("r", 4, 0, 2), ("r", 5, 0, 3), ("s", 1, 3), ("f", 1, 0), ("f", 3, 1), ("f", 6, 0), ("r", 4, 0, 3), ("f", 2, 2), ("f", 1, 1), ("s", 2, 3), ("f", 5, 0), ("f", 6, 1), ("f", 2, 3), ("f", 5, 1), ("f", 3, 2), ("f", 1, 2), ("s", 1, 4), ("f", 6, 2), ("f", 3, 3), ("f", 5, 2), ("f", 1, 3), ("f", 6, 3), ("f", 4, 0), ("f", 5, 3), ("s", 2, 4), ("f", 4, 1), ("f", 4, 2), ("f", 4, 3),),
 }
 
 def layer_kernel(

time: 165 us -> 165 us (level)
  no operation moved by 1% of the time
where the time goes in v5:
time: 165 us
  Pallas kernels  150 us (91%)
  other arithmetic  7.75 us (5%)
  local copies, waits for them, and re-layouts  6.53 us (4%)
    pallas_call x1, Pallas kernels, per_device(): pl.pallas_call(lambda *refs: layer_kernel(n_batch, n_head, *refs), out_sh...  150 us

profile of v5, /device:TPU:1, one launch (start us, length us, event | category | flops | bytes accessed | tf_op | source)
XLA Modules:
  0.0 164.5 jit_solution(4405589727892640981)
XLA Ops:
  0.7 2.4 %pad_maximum_fusion.refs_8_ = bf16[4,192,768]{2,1,0:T(8,128)(2,1)} fusion(bf16[1,192,768]{2,1,0:T(8,128)(2,1)} %bitcast.40, bf16[1,192,768]{2,1,0:T(8,128)(2,1)} %bitcast.41, bf16[1,192,768]{2,1,0:T(8,128)(2,1)} %bitcast.42, bf16[1,192,768]{2,1,0:T(8,128)(2,1)} %bitcast.43), kind=kLoop, calls=%fused_computation | loop fusion | flops 1769472 | bytes 2359296 | tf_op jit(solution)/shard_map/stack | solution.py:999
  3.0 149.6 %shard_map.357 = (bf16[512,768]{1,0:T(8,128)(2,1)}, bf16[512,768]{1,0:T(8,128)(2,1)}, bf16[3,192,768]{2,1,0:T(8,128)(2,1)}, bf16[1,192,768]{2,1,0:T(8,128)(2,1)}...) custom-call(s32[4]{0:T(128)} %refs_0_.1, s32[4]{0:T(128)} %refs_1_.1, ...), custom_call_target="tpu_custom_call" | custom-call | tf_op jit(solution)/shard_map/pallas_call | solution.py:1016
  152.6 1.3 fusion
  153.9 1.7 %slice_reduce_fusion = (f32[768]{0:T(1024)}, f32[768]{0:T(1024)}, f32[768]{0:T(1024)}, f32[768]{0:T(1024)}, f32[768]{0:T(1024)}, /*index=5*/f32[768]{0:T(1024)}, f32[768]{0:T(1024)}) fusion(f32[16,768]{1,0:T(8,128)} %get-tuple-element.28), kind=kLoop, calls=%fused_computation.9 | loop fusion | bytes 43008 | tf_op jit(solution)/shard_map/slice | solution.py:1070
  155.6 1.3 slice_bitcast_fusion
  156.8 0.0 copy-start
  156.8 2.8 %convert_bitcast_fusion = (f32[768,192]{0,1:T(8,128)}, f32[768,192]{0,1:T(8,128)}, f32[768,192]{0,1:T(8,128)}, f32[192,768]{1,0:T(8,128)}) fusion(bf16[3,192,768]{2,1,0:T(8,128)(2,1)} %get-tuple-element.29, bf16[1,192,768]{2,1,0:T(8,128)(2,1)} %get-tuple-element.30), kind=kLoop, calls=%fused_computation.3 | loop fusion | flops 589824 | bytes 3538944 | tf_op jit(solution)/shard_map/convert_element_type | solution.py:1067
  159.7 0.0 copy-done
  159.7 0.0 copy-start.2
  159.7 2.5 %bitcast_convert_fusion = (f32[768,768]{1,0:T(8,128)}, f32[768,768]{1,0:T(8,128)}) fusion(bf16[2,768,768]{2,1,0:T(8,128)(2,1)S(1)} %copy-done), kind=kLoop, calls=%fused_computation.1 | loop fusion | flops 1179648 | bytes 7077888 | tf_op jit(solution)/shard_map/convert_element_type | solution.py:1070
  162.2 0.0 copy-start.1
  162.2 0.0 copy-done.2
  162.2 0.9 copy.43
  163.1 0.5 copy-done.1
  163.6 0.9 copy.44
Async XLA Ops:
  156.8 2.8 %copy-start = (bf16[2,768,768]{2,1,0:T(8,128)(2,1)S(1)}, bf16[2,768,768]{2,1,0:T(8,128)(2,1)}, u32[]{:S(2)}) copy-start(bf16[2,768,768]{2,1,0:T(8,128)(2,1)} %get-tuple-element.31) | copy-start | bytes 7077892
  159.7 2.6 %copy-start.2 = (bf16[512,768]{1,0:T(8,128)(2,1)S(1)}, bf16[512,768]{1,0:T(8,128)(2,1)}, u32[]{:S(2)}) copy-start(bf16[512,768]{1,0:T(8,128)(2,1)} %get-tuple-element.69) | copy-start | bytes 2359300
  162.2 1.4 copy-start.1
